TPU v7x, 128 devices: a whole 4x4x4 slice. The times are simulated.
128 devices in a mesh: sub: 8 (over z, core), row: 16 (over x, y).
Axes of the slice: x: 4, y: 4, z: 4, core: 2. Of those that a mesh axis runs over, the one named last changes fastest.
Arguments:
- spectra: bfloat16 [8, 131072, 256], P('sub', 'row')
- mass_blocks: bfloat16 [8, 1024, 9, 128, 128], P('sub', 'row'), may hold values from -0.1875 to 0.1875
- offsets: int32 [8, 1024, 9], P('sub', 'row'), may hold values from -16 to 16
- counts: int32 [8], P('sub'), may hold values from 1 to 131072, 734003 in all
Outputs:
- weighted_modes: bfloat16 [8, 131072, 192], P('sub', 'row')
Inputs may be any that keep to these rules, and one draw needn't show every extreme that they name: `counts`: rows at or past a subdomain's count hold no data; the largest count is exactly 131072.
All inputs are finite; a program needn't handle non-finite values. No bound on the sum of `counts` on one device may be relied on, other than what follows from the above.
Results may differ from a plain program's by a relative error of at most 0.001.
The roundings to bfloat16 on the way count: a program that leaves them out, or rounds other values in their place, can miss the bound.
Values may be sent and summed in bfloat16 or wider, within the bound.
No kernel may reach another device: no remote copies, remote signals or barrier semaphores. Data moves between devices by JAX's collectives and lax.ppermute only.
A program may use at most 256 MiB of HBM per device.

v0:
```python
import jax
import jax.numpy as jnp
from jax import lax
from jax.sharding import Mesh
from jax.sharding import PartitionSpec as P

RANK = 48
FREQ = 2
ITERS = 5
HB = 16
SUB = ("sub_0", "sub_1")


def with_halo(value, sides, width):
    for axis, dim in sides:
        devices, length = (lax.axis_size(axis), value.shape[dim])
        up = [(i, (i + 1) % devices) for i in range(devices - 1)]
        down = [(j, i) for i, j in up]
        last = lax.slice_in_dim(value, length - width, length, axis=dim)
        initial = lax.slice_in_dim(value, 0, width, axis=dim)
        before = lax.ppermute(last, axis, up)
        after = lax.ppermute(initial, axis, down)
        value = jnp.concatenate([before, value, after], axis=dim)
    return value


def copy_for_each(value, axis):
    devices = lax.axis_size(axis)
    return lax.all_to_all(
        jnp.broadcast_to(value[None], (devices, *value.shape)), axis, 0, 0, tiled=True
    )


def over_copies(value, axis):
    everything = copy_for_each(value, axis)
    return jnp.sum(everything, axis=0)


def merged_by_axis(value, axes, combine):
    for axis in axes:
        pieces = lax.all_gather(value, axis)
        value = pieces[0]
        for k in range(1, lax.axis_size(axis)):
            value = combine(value, pieces[k])
    return value


def add_states(first, second):
    return first + second


def whiten(gram, rank_kept, iterations):
    half_width = gram.shape[1] // 2
    g_real = gram[:, :half_width, :half_width] + gram[:, half_width:, half_width:]
    g_imag = gram[:, :half_width, half_width:] - gram[:, half_width:, :half_width]
    realified = jnp.concatenate(
        [jnp.concatenate([g_real, -g_imag], 2), jnp.concatenate([g_imag, g_real], 2)], 1
    )
    scaled = realified / jnp.sqrt(
        jnp.sum(realified * realified, axis=(1, 2), keepdims=True) + 1e-06
    )
    identity = jnp.broadcast_to(jnp.eye(2 * half_width, dtype=jnp.float32), scaled.shape)
    iterate = scaled
    whitener = identity
    for step in range(iterations):
        correction = 1.5 * identity - 0.5 * jnp.einsum(
            "fij,fjk->fik", whitener, iterate, precision=lax.Precision.HIGHEST
        )
        iterate = jnp.einsum("fij,fjk->fik", iterate, correction, precision=lax.Precision.HIGHEST)
        whitener = jnp.einsum("fij,fjk->fik", correction, whitener, precision=lax.Precision.HIGHEST)
    r_real = whitener[:, :half_width, :rank_kept]
    r_imag = whitener[:, half_width:, :rank_kept]
    projector = jnp.concatenate(
        [jnp.concatenate([r_real, r_imag], 2), jnp.concatenate([-r_imag, r_real], 2)], 1
    )
    return projector.astype(jnp.bfloat16)


def weigh_columns(padded, mass_local, block_index, live_rows, reach):
    row_count = live_rows.shape[0]
    block_size = mass_local.shape[2]
    slot_count = mass_local.shape[1]
    block_count = row_count // block_size
    col_count = padded.shape[1]
    blocks = padded.reshape(block_count + 2 * reach, block_size, col_count)
    summed = jnp.zeros((block_count, block_size, col_count), jnp.float32)
    for slot in range(slot_count):
        picked = jnp.take(blocks, block_index[:, slot], axis=0)
        summed = summed + jnp.einsum(
            "bij,bjc->bic", mass_local[:, slot], picked, preferred_element_type=jnp.float32
        )
    return jnp.where(live_rows, summed.reshape(row_count, col_count), 0.0).astype(jnp.bfloat16)


def local(spectra, mass_blocks, offsets, counts):
    row_count = spectra.shape[1]
    col_count = spectra.shape[2]
    block_size = mass_blocks.shape[3]
    reach = HB
    freq_count = FREQ
    first_row = lax.axis_index("row") * row_count
    live_rows = (first_row + jnp.arange(row_count, dtype=jnp.int32) < counts[0])[:, None]
    masked = jnp.where(live_rows, spectra[0], jnp.zeros((), spectra.dtype))
    block_index = jnp.arange(row_count // block_size, dtype=jnp.int32)[:, None] + offsets[0] + reach
    padded = with_halo(masked, (("row", 0),), reach * block_size)
    weighted = weigh_columns(padded, mass_blocks[0], block_index, live_rows, reach)
    columns = weighted.reshape(row_count, freq_count, col_count // freq_count)
    gram = jnp.einsum("rfc,rfd->fcd", columns, columns, preferred_element_type=jnp.float32)
    partial_gram = over_copies(gram, "row")
    combined = merged_by_axis(partial_gram, SUB, add_states)
    projector = whiten(combined, RANK, ITERS)
    modes = jnp.einsum("rfc,fcd->rfd", columns, projector, preferred_element_type=jnp.float32)
    return modes.reshape(1, row_count, freq_count * 2 * RANK).astype(jnp.bfloat16)


def solution(mesh):
    finer = Mesh(mesh.devices.reshape(4, 2, mesh.shape["row"]), ("sub_0", "sub_1", "row"))
    return jax.shard_map(
        local,
        mesh=finer,
        in_specs=(
            P(SUB, "row", None),
            P(SUB, "row", None, None, None),
            P(SUB, "row", None),
            P(SUB),
        ),
        out_specs=P(SUB, "row", None),
        check_vma=False,
    )
```

profile of v0, /device:TPU:0, one launch (start us, length us, event | category | flops | bytes accessed | tf_op | source)
XLA Modules:
  0.0 269.2 jit_solution(13110517636446932603)
XLA Ops:
  0.7 6.0 %bitcast_select_fusion = bf16[8192,256]{1,0:T(8,128)(2,1)S(1)} fusion(bf16[1,8192,256]{2,1,0:T(8,128)(2,1)} %param.6, pred[8192]{0:T(1024)(128)(4,1)S(1)} %add_compare_fusion), kind=kLoop, calls=%fused_computation.14 | loop fusion | flops 2097152 | bytes 8396800 | tf_op jit(solution)/shard_map/jit(_where)/select_n | solution.py:103
  6.8 3.7 %collective-permute-start = (bf16[2048,256]{1,0:T(8,128)(2,1)S(1)}, bf16[2048,256]{1,0:T(8,128)(2,1)S(1)}, u32[]{:S(2)}, u32[]{:S(2)}) collective-permute-start(bf16[2048,256]{1,0:T(8,128)(2,1)S(1)} %get-tuple-element.26), channel_id=1, source_target_pairs={{0,1},{1,2},{2,3},{3,4},{4,5},{5,6},{6,7},{7,8},{8,9},{9,10},{10,1... | collective-permute-start | bytes 3145736 | tf_op jit(solution)/shard_map/ppermute | solution.py:21
  11.8 17.0 %copy.65 = bf16[1,64,9,128,128]{4,3,1,2,0:T(8,128)(2,1)} copy(bf16[1,64,9,128,128]{4,3,2,1,0:T(8,128)(2,1)} %param.7) | data formatting | bytes 37748736 | tf_op args[1]
  28.8 3.9 %collective-permute-done = bf16[2048,256]{1,0:T(8,128)(2,1)S(1)} collective-permute-done((bf16[2048,256]{1,0:T(8,128)(2,1)S(1)}, bf16[2048,256]{1,0:T(8,128)(2,1)S(1)}, u32[]{:S(2)}, u32[]{:S(2)}) %collective-permute-start) | collective-permute-done | bytes 1048608 | tf_op jit(solution)/shard_map/ppermute | solution.py:21
  32.8 4.2 %collective-permute-done.1 = bf16[2048,256]{1,0:T(8,128)(2,1)S(1)} collective-permute-done((bf16[2048,256]{1,0:T(8,128)(2,1)S(1)}, bf16[2048,256]{1,0:T(8,128)(2,1)S(1)}, u32[]{:S(2)}, u32[]{:S(2)}) %collective-permute-start.1) | collective-permute-done | bytes 1048608 | tf_op jit(solution)/shard_map/ppermute | solution.py:22
  37.0 23.2 %pad_maximum_fusion = bf16[12288,256]{1,0:T(8,128)(2,1)} fusion(bf16[2048,256]{1,0:T(8,128)(2,1)S(1)} %collective-permute-done.1, bf16[8192,256]{1,0:T(8,128)(2,1)S(1)} %bitcast_select_fusion, bf16[2048,256]{1,0:T(8,128)(2,1)S(1)} %collective-permute-done), kind=kLoop, calls=%fused_computation.13 | loop fusion | flops 18874368 | bytes 12582912 | tf_op jit(solution)/shard_map/concatenate | solution.py:23
  60.1 5.7 %gather_fusion.8 = bf16[64,128,256]{2,1,0:T(8,128)(2,1)} fusion(bf16[96,128,256]{2,1,0:T(8,128)(2,1)} %bitcast.119, s32[1024]{0:T(1024)S(1)} %get-tuple-element.47), kind=kCustom, calls=%fused_computation.8.clone | custom fusion | bytes 8388864 | tf_op jit(solution)/shard_map/jit(_take)/gather | solution.py:88
  65.8 5.7 %gather_fusion.7 = bf16[64,128,256]{2,1,0:T(8,128)(2,1)} fusion(bf16[96,128,256]{2,1,0:T(8,128)(2,1)} %bitcast.120, s32[1024]{0:T(1024)S(1)} %get-tuple-element.48), kind=kCustom, calls=%fused_computation.7.clone | custom fusion | bytes 8388864 | tf_op jit(solution)/shard_map/jit(_take)/gather | solution.py:88
  71.5 5.5 %gather_fusion.6 = bf16[64,128,256]{2,1,0:T(8,128)(2,1)} fusion(bf16[96,128,256]{2,1,0:T(8,128)(2,1)} %bitcast.121, s32[1024]{0:T(1024)S(1)} %get-tuple-element.49), kind=kCustom, calls=%fused_computation.6.clone | custom fusion | bytes 8388864 | tf_op jit(solution)/shard_map/jit(_take)/gather | solution.py:88
  77.0 5.7 %gather_fusion.5 = bf16[64,128,256]{2,1,0:T(8,128)(2,1)} fusion(bf16[96,128,256]{2,1,0:T(8,128)(2,1)} %bitcast.122, s32[1024]{0:T(1024)S(1)} %get-tuple-element.50), kind=kCustom, calls=%fused_computation.5.clone | custom fusion | bytes 8388864 | tf_op jit(solution)/shard_map/jit(_take)/gather | solution.py:88
  82.7 5.6 %gather_fusion.4 = bf16[64,128,256]{2,1,0:T(8,128)(2,1)} fusion(bf16[96,128,256]{2,1,0:T(8,128)(2,1)} %bitcast.123, s32[1024]{0:T(1024)S(1)} %get-tuple-element.51), kind=kCustom, calls=%fused_computation.4.clone | custom fusion | bytes 8388864 | tf_op jit(solution)/shard_map/jit(_take)/gather | solution.py:88
  88.3 5.7 %gather_fusion.3 = bf16[64,128,256]{2,1,0:T(8,128)(2,1)} fusion(bf16[96,128,256]{2,1,0:T(8,128)(2,1)} %bitcast.124, s32[1024]{0:T(1024)S(1)} %get-tuple-element.52), kind=kCustom, calls=%fused_computation.3.clone | custom fusion | bytes 8388864 | tf_op jit(solution)/shard_map/jit(_take)/gather | solution.py:88
  94.0 5.6 %gather_fusion.2 = bf16[64,128,256]{2,1,0:T(8,128)(2,1)} fusion(bf16[96,128,256]{2,1,0:T(8,128)(2,1)} %bitcast.125, s32[1024]{0:T(1024)S(1)} %get-tuple-element.53), kind=kCustom, calls=%fused_computation.2.clone | custom fusion | bytes 8388864 | tf_op jit(solution)/shard_map/jit(_take)/gather | solution.py:88
  99.5 5.6 %gather_fusion.1 = bf16[64,128,256]{2,1,0:T(8,128)(2,1)} fusion(bf16[96,128,256]{2,1,0:T(8,128)(2,1)} %bitcast.126, s32[1024]{0:T(1024)S(1)} %get-tuple-element.54), kind=kCustom, calls=%fused_computation.1.clone | custom fusion | bytes 8388864 | tf_op jit(solution)/shard_map/jit(_take)/gather | solution.py:88
  105.1 5.7 %gather_fusion = bf16[64,128,256]{2,1,0:T(8,128)(2,1)} fusion(bf16[96,128,256]{2,1,0:T(8,128)(2,1)} %bitcast.127, s32[1024]{0:T(1024)S(1)} %pad_clamp_fusion.8), kind=kCustom, calls=%fused_computation.clone | custom fusion | bytes 8388864 | tf_op jit(solution)/shard_map/jit(_take)/gather | solution.py:88
  110.8 8.5 %fusion.2 = f32[64,256,128]{2,1,0:T(8,128)} fusion(bf16[64,128,256]{2,1,0:T(8,128)(2,1)} %gather_fusion.7, pred[64]{0:T(512)(128)(4,1)S(1)} %get-tuple-element.31, bf16[64,9,128,128]{3,2,0,1:T(8,128)(2,1)} %bitcast.128), kind=kOutput, calls=%fused_computation.17 | convolution fusion | flops 538968064 | bytes 14680128 | tf_op jit(solution)/shard_map/bij,bjc->bic/dot_general | solution.py:89
  119.4 6.4 %fusion.4 = f32[64,256,128]{2,1,0:T(8,128)} fusion(bf16[64,128,256]{2,1,0:T(8,128)(2,1)S(1)} %copy-done.3, pred[64]{0:T(512)(128)(4,1)S(1)} %get-tuple-element.33, bf16[64,9,128,128]{3,2,0,1:T(8,128)(2,1)} %bitcast.129), kind=kOutput, calls=%fused_computation.19 | convolution fusion | flops 538968064 | bytes 14680128 | tf_op jit(solution)/shard_map/bij,bjc->bic/dot_general | solution.py:89
  125.8 7.8 %fusion.6 = f32[64,256,128]{2,1,0:T(8,128)} fusion(bf16[64,128,256]{2,1,0:T(8,128)(2,1)} %gather_fusion.5, pred[64]{0:T(512)(128)(4,1)S(1)} %get-tuple-element.35, bf16[64,9,128,128]{3,2,0,1:T(8,128)(2,1)} %bitcast.130), kind=kOutput, calls=%fused_computation.21 | convolution fusion | flops 538968064 | bytes 14680128 | tf_op jit(solution)/shard_map/bij,bjc->bic/dot_general | solution.py:89
  133.6 4.7 %fusion.8 = f32[64,256,128]{2,1,0:T(8,128)} fusion(bf16[64,128,256]{2,1,0:T(8,128)(2,1)S(1)} %copy-done.2, pred[64]{0:T(512)(128)(4,1)S(1)} %get-tuple-element.37, bf16[64,9,128,128]{3,2,0,1:T(8,128)(2,1)S(1)} %bitcast.134), kind=kOutput, calls=%fused_computation.23 | convolution fusion | flops 538968064 | bytes 14680576 | tf_op jit(solution)/shard_map/bij,bjc->bic/dot_general | solution.py:89
  138.4 7.1 %fusion.10 = f32[64,256,128]{2,1,0:T(8,128)} fusion(bf16[64,128,256]{2,1,0:T(8,128)(2,1)} %gather_fusion.3, pred[64]{0:T(512)(128)(4,1)S(1)} %get-tuple-element.39, bf16[64,9,128,128]{3,2,0,1:T(8,128)(2,1)S(1)} %bitcast.135), kind=kOutput, calls=%fused_computation.25 | convolution fusion | flops 538968064 | bytes 14680576 | tf_op jit(solution)/shard_map/bij,bjc->bic/dot_general | solution.py:89
  145.5 4.6 %fusion.12 = f32[64,256,128]{2,1,0:T(8,128)} fusion(bf16[64,128,256]{2,1,0:T(8,128)(2,1)S(1)} %copy-done.1, pred[64]{0:T(512)(128)(4,1)S(1)} %get-tuple-element.41, bf16[64,9,128,128]{3,2,0,1:T(8,128)(2,1)S(1)} %bitcast.136), kind=kOutput, calls=%fused_computation.27 | convolution fusion | flops 538968064 | bytes 14680576 | tf_op jit(solution)/shard_map/bij,bjc->bic/dot_general | solution.py:89
  150.1 7.3 %fusion.14 = f32[64,256,128]{2,1,0:T(8,128)} fusion(bf16[64,128,256]{2,1,0:T(8,128)(2,1)} %gather_fusion.1, pred[64]{0:T(512)(128)(4,1)S(1)} %get-tuple-element.43, bf16[64,9,128,128]{3,2,0,1:T(8,128)(2,1)S(1)} %bitcast.137), kind=kOutput, calls=%fused_computation.29 | convolution fusion | flops 538968064 | bytes 14680576 | tf_op jit(solution)/shard_map/bij,bjc->bic/dot_general | solution.py:89
  157.4 4.8 %fusion.16 = f32[64,256,128]{2,1,0:T(8,128)} fusion(bf16[64,128,256]{2,1,0:T(8,128)(2,1)S(1)} %copy-done, pred[64]{0:T(512)(128)(4,1)S(1)} %get-tuple-element.45, bf16[64,9,128,128]{3,2,0,1:T(8,128)(2,1)S(1)} %bitcast.138), kind=kOutput, calls=%fused_computation.31 | convolution fusion | flops 538968064 | bytes 14680576 | tf_op jit(solution)/shard_map/bij,bjc->bic/dot_general | solution.py:89
  162.2 25.7 %add_bitcast_fusion = bf16[64,128,256]{1,2,0:T(8,128)(2,1)} fusion(f32[64,256,128]{2,1,0:T(8,128)} %fusion.2, f32[64,256,128]{2,1,0:T(8,128)} %fusion.4, f32[64,256,128]{2,1,0:T(8,128)} %fusion.6, f32[64,256,128]{2,1,0:T(8,128)} %fusion.8, f32[64,256,128]{2,1,0:T(8,128)} %fusion.10, f32[64,256,128]{2,1,0:T(8,128)} %fusion.12, f32[64,256,128]{2,1,0:T(8,128)} %fusion.16, ...), kind=kOutput, calls=%fused_computation.11 | convolution fusion | flops 557842432 | bytes 77594688 | tf_op jit(solution)/shard_map/bij,bjc->bic/dot_general | solution.py:89
  187.9 6.8 %copy.46 = bf16[64,128,256]{1,0,2:T(8,128)(2,1)} copy(bf16[64,128,256]{1,2,0:T(8,128)(2,1)} %add_bitcast_fusion) | data formatting | bytes 8388608 | tf_op jit(solution)/shard_map/add | solution.py:89
  194.7 7.3 %reshape.46 = bf16[8192,2,128]{0,2,1:T(8,128)(2,1)} reshape(bf16[64,128,256]{1,0,2:T(8,128)(2,1)} %copy.46) | data formatting | bytes 8388608 | tf_op jit(solution)/shard_map/reshape | solution.py:92
  202.0 4.7 %fusion.38 = f32[2,128,128]{2,1,0:T(8,128)S(1)} fusion(bf16[8192,2,128]{0,2,1:T(8,128)(2,1)} %reshape.46, pred[8192]{0:T(1024)(128)(4,1)S(1)} %add_compare_fusion), kind=kOutput, calls=%fused_computation.60 | convolution fusion | flops 538968064 | bytes 4333568 | tf_op jit(solution)/shard_map/rfc,rfd->fcd/dot_general | solution.py:108
  208.3 8.2 %all-to-all-start = ((f32[16,2,128,128]{3,2,1,0:T(8,128)}), f32[16,2,128,128]{3,2,1,0:T(8,128)S(1)}, u32[]{:S(2)}, u32[]{:S(2)}) async-start(f32[16,2,128,128]{3,2,1,0:T(8,128)} %broadcast_in_dim.63), calls=%async_computation | async-start | bytes 4194304 | tf_op jit(solution)/shard_map/all_to_all | solution.py:29
  216.5 28.6 %all-to-all-done = f32[16,2,128,128]{3,2,1,0:T(8,128)S(1)} async-done(((f32[16,2,128,128]{3,2,1,0:T(8,128)}), f32[16,2,128,128]{3,2,1,0:T(8,128)S(1)}, u32[]{:S(2)}, u32[]{:S(2)}) %all-to-all-start) | async-done | bytes 2097184 | tf_op jit(solution)/shard_map/all_to_all | solution.py:29
  245.2 14.2 %all-gather = f32[8,128,128]{2,1,0:T(8,128)S(1)} all-gather(f32[2,128,128]{2,1,0:T(8,128)S(1)} %reduce_sum.18), channel_id=2, replica_groups=mesh['sub_0'=4,'sub_1'=2,'row'=16] {'sub_0'}, dimensions={0}, use_global_device_ids=true | all-gather | bytes 655360 | tf_op jit(solution)/shard_map/all_gather | solution.py:41
  259.5 2.4 all_gather.12
  266.5 2.7 %convolution_convert_fusion = bf16[2,96,8192]{2,1,0:T(8,128)(2,1)} fusion(bf16[8192,2,128]{0,2,1:T(8,128)(2,1)S(1)} %copy-done.4, pred[8192]{0:T(1024)(128)(4,1)S(1)} %add_compare_fusion, bf16[2,64,48]{1,2,0:T(8,128)(2,1)S(1)} %get-tuple-element.29, bf16[2,64,48]{1,2,0:T(8,128)(2,1)S(1)} %negate_convert_fusion, bf16[2,64,48]{1,2,0:T(8,128)(2,1)S(1)} %get-tuple-element.28), kind=kOutput, calls=%fused_computation.10 | convolution fusion | flops 406519808 | bytes 7385088 | tf_op jit(solution)/shard_map/rfc,fcd->rfd/dot_general | solution.py:112
  (58 shorter events, 7.7 us)
Async XLA Ops:
  6.8 26.0 %collective-permute-start = (bf16[2048,256]{1,0:T(8,128)(2,1)S(1)}, bf16[2048,256]{1,0:T(8,128)(2,1)S(1)}, u32[]{:S(2)}, u32[]{:S(2)}) collective-permute-start(bf16[2048,256]{1,0:T(8,128)(2,1)S(1)} %get-tuple-element.26), channel_id=1, source_target_pairs={{0,1},{1,2},{2,3},{3,4},{4,5},{5,6},{6,7},{7,8},{8,9},{9,10},{10,1... | collective-permute-start | bytes 3145736 | tf_op jit(solution)/shard_map/ppermute | solution.py:21
  10.5 18.3 %copy-start.5 = (s32[1,64,9]{1,0,2:T(1,128)S(1)}, s32[1,64,9]{1,0,2:T(1,128)}, u32[]{:S(2)}) copy-start(s32[1,64,9]{1,0,2:T(1,128)} %param.8) | copy-start | bytes 6916
  10.5 26.5 %collective-permute-start.1 = (bf16[2048,256]{1,0:T(8,128)(2,1)S(1)}, bf16[2048,256]{1,0:T(8,128)(2,1)S(1)}, u32[]{:S(2)}, u32[]{:S(2)}) collective-permute-start(bf16[2048,256]{1,0:T(8,128)(2,1)S(1)} %get-tuple-element.27), channel_id=1, source_target_pairs={{1,0},{2,1},{3,2},{4,3},{5,4},{6,5},{7,6},{8,7},{9,8},{10,9},{11,1... | collective-permute-start | bytes 3145736 | tf_op jit(solution)/shard_map/ppermute | solution.py:22
  110.8 8.5 %copy-start.3 = (bf16[64,128,256]{2,1,0:T(8,128)(2,1)S(1)}, bf16[64,128,256]{2,1,0:T(8,128)(2,1)}, u32[]{:S(2)}) copy-start(bf16[64,128,256]{2,1,0:T(8,128)(2,1)} %gather_fusion.6) | copy-start | bytes 12582916
  110.8 22.7 %slice-start = ((s8[18874368]{0:T(1024)(128)(4,1)}), s8[4194304]{0:T(1024)(128)(4,1)S(1)}, s32[]{:S(2)}) async-start(s8[18874368]{0:T(1024)(128)(4,1)} %bitcast.132), calls=%async_computation.1 | async-start | bytes 8388608
  110.8 22.7 %slice-start.1 = ((s8[18874368]{0:T(1024)(128)(4,1)}), s8[4194304]{0:T(1024)(128)(4,1)S(1)}, s32[]{:S(2)}) async-start(s8[18874368]{0:T(1024)(128)(4,1)} %bitcast.132), calls=%async_computation.2 | async-start | bytes 8388608
  119.4 14.2 %slice-start.2 = ((s8[18874368]{0:T(1024)(128)(4,1)}), s8[4194304]{0:T(1024)(128)(4,1)S(1)}, s32[]{:S(2)}) async-start(s8[18874368]{0:T(1024)(128)(4,1)} %bitcast.132), calls=%async_computation.3 | async-start | bytes 8388608
  119.4 14.2 %slice-start.3 = ((s8[18874368]{0:T(1024)(128)(4,1)}), s8[4194304]{0:T(1024)(128)(4,1)S(1)}, s32[]{:S(2)}) async-start(s8[18874368]{0:T(1024)(128)(4,1)} %bitcast.132), calls=%async_computation.4 | async-start | bytes 8388608
  125.8 7.8 %slice-start.4 = ((s8[18874368]{0:T(1024)(128)(4,1)}), s8[2097152]{0:T(1024)(128)(4,1)S(1)}, s32[]{:S(2)}) async-start(s8[18874368]{0:T(1024)(128)(4,1)} %bitcast.132), calls=%async_computation.5 | async-start | bytes 4194304
  125.8 7.8 %copy-start.2 = (bf16[64,128,256]{2,1,0:T(8,128)(2,1)S(1)}, bf16[64,128,256]{2,1,0:T(8,128)(2,1)}, u32[]{:S(2)}) copy-start(bf16[64,128,256]{2,1,0:T(8,128)(2,1)} %gather_fusion.4) | copy-start | bytes 12582916
  138.4 7.1 %copy-start.1 = (bf16[64,128,256]{2,1,0:T(8,128)(2,1)S(1)}, bf16[64,128,256]{2,1,0:T(8,128)(2,1)}, u32[]{:S(2)}) copy-start(bf16[64,128,256]{2,1,0:T(8,128)(2,1)} %gather_fusion.2) | copy-start | bytes 12582916
  150.1 7.3 %copy-start = (bf16[64,128,256]{2,1,0:T(8,128)(2,1)S(1)}, bf16[64,128,256]{2,1,0:T(8,128)(2,1)}, u32[]{:S(2)}) copy-start(bf16[64,128,256]{2,1,0:T(8,128)(2,1)} %gather_fusion) | copy-start | bytes 12582916
  208.3 36.8 %all-to-all-start = ((f32[16,2,128,128]{3,2,1,0:T(8,128)}), f32[16,2,128,128]{3,2,1,0:T(8,128)S(1)}, u32[]{:S(2)}, u32[]{:S(2)}) async-start(f32[16,2,128,128]{3,2,1,0:T(8,128)} %broadcast_in_dim.63), calls=%async_computation | async-start | bytes 4194304 | tf_op jit(solution)/shard_map/all_to_all | solution.py:29
  259.5 7.0 %copy-start.4 = (bf16[8192,2,128]{0,2,1:T(8,128)(2,1)S(1)}, bf16[8192,2,128]{0,2,1:T(8,128)(2,1)}, u32[]{:S(2)}) copy-start(bf16[8192,2,128]{0,2,1:T(8,128)(2,1)} %reshape.46) | copy-start | bytes 12582916
where the time goes:
time: 271 us; the launch traced here: 269 us
  matrix products  88.4 us (33%)
  local copies, waits for them, and re-layouts  83.6 us (31%)
  waiting for transfers between devices  36.7 us (14%)
  other arithmetic  29.7 us (11%)
  blocking collectives  16.6 us (6%)
  starting transfers between devices  13.1 us (5%)
    dot_general x9, matrix products, weigh_columns(): jnp.einsum('bij,bjc->bic', mass_local[:, slot], picked, preferred_element...  76.9 us
    gather x9, local copies, waits for them, and re-layouts, weigh_columns(): picked = jnp.take(blocks, block_index[:, slot], axis=0)  50.7 us
    all_to_all x1, waiting for transfers between devices, copy_for_each(): lax.all_to_all(jnp.broadcast_to(value[None], (devices, *value.shape)), ax...  28.6 us
    concatenate x1, other arithmetic, with_halo(): value = jnp.concatenate([before, value, after], axis=dim)  23.2 us
    unnamed x23, local copies, waits for them, and re-layouts  17 us
    all_gather x2, blocking collectives, merged_by_axis(): pieces = lax.all_gather(value, axis)  16.6 us
    all_to_all x1, starting transfers between devices, copy_for_each(): lax.all_to_all(jnp.broadcast_to(value[None], (devices, *value.shape)), ax...  8.18 us
    reshape x1, local copies, waits for them, and re-layouts, weigh_columns(): summed.reshape(row_count, col_count)  7.32 us
  transfers between devices with their start and end apart: 3, of which 3 were waited for; matrix products, arithmetic and copies ran while one was open for 6% of the time, Pallas kernels for 0%

commit v1 on v0

v1 whole, which is shorter than its diff:
```python
import functools

import jax
import jax.numpy as jnp
from jax import lax
from jax.experimental import pallas as pl
from jax.experimental.pallas import tpu as pltpu
from jax.sharding import Mesh
from jax.sharding import PartitionSpec as P

BLK = 64
RANK = 48
FREQ = 2
ITERS = 5
HB = 16
BS = 128
GROUP = 4
CHUNK = 1024
SUB = ("z", "c")
ROW = ("x", "y")


def fill_blocks(rel, copies, xs, lo, hi):
    for copy in copies:
        copy.start()
    spare = xs.shape[0] - 1
    xs[spare] = jnp.zeros(xs.shape[1:], xs.dtype)
    for copy in copies:
        copy.wait()
    end = rel + HB * BS
    cut = lax.shift_right_arithmetic(end, 7)
    kept = jnp.bitwise_and(end, BS - 1)

    @pl.when((kept > 0) & (cut >= lo) & (cut < hi))
    def _():
        rows = lax.broadcasted_iota(jnp.int32, xs.shape[1:], 0)
        block = xs[cut]
        xs[cut] = jnp.where(rows < kept, block, jnp.zeros_like(block))


def weigh_group(idx_ref, rel, first, mass_ref, xs, zt_ref, gram):
    slots = mass_ref.shape[1]
    rows = lax.broadcasted_iota(jnp.int32, (BS, xs.shape[2]), 0)
    parts = []
    for r in range(mass_ref.shape[0]):
        b = first + r
        left = jnp.concatenate([mass_ref[r, k] for k in range(slots)], axis=1)
        right = jnp.concatenate([xs[idx_ref[k, b]] for k in range(slots)], axis=0)
        acc = jnp.dot(left, right, preferred_element_type=jnp.float32)
        parts.append(jnp.where(rows < rel - b * BS, acc, 0.0).astype(jnp.bfloat16))
    z = jnp.concatenate(parts, axis=0)
    zt = z.T
    zt_ref[...] = zt
    for f in range(FREQ):
        s = slice(f * 2 * BLK, (f + 1) * 2 * BLK)
        gram[f] += jnp.dot(zt[s], z[:, s], preferred_element_type=jnp.float32)


def inner_kernel(idx_ref, rel_ref, mass_ref, sp_ref, zt_ref, gram_ref, xs, sem):
    step = pl.program_id(0)
    rel = rel_ref[0]
    local = sp_ref.shape[0]

    @pl.when(step == 0)
    def _():
        gram_ref[...] = jnp.zeros_like(gram_ref)
        copies = [pltpu.make_async_copy(sp_ref, xs.at[pl.ds(HB, local)], sem.at[0])]
        fill_blocks(rel, copies, xs, HB, HB + local)

    weigh_group(idx_ref, rel, HB + step * GROUP, mass_ref, xs, zt_ref, gram_ref)


def edge_kernel(idx_ref, rel_ref, mass_ref, sp_ref, prev_ref, next_ref, part_ref, zt_in, zt_ref, packed_ref, xs, gram, sem):
    del zt_in
    step = pl.program_id(0)
    rel = rel_ref[0]
    local = sp_ref.shape[0]
    half = HB // GROUP

    @pl.when(step == 0)
    def _():
        gram[...] = part_ref[...]
        copies = [
            pltpu.make_async_copy(prev_ref, xs.at[pl.ds(0, HB)], sem.at[0]),
            pltpu.make_async_copy(sp_ref, xs.at[pl.ds(HB, local)], sem.at[1]),
            pltpu.make_async_copy(next_ref, xs.at[pl.ds(HB + local, HB)], sem.at[2]),
        ]
        fill_blocks(rel, copies, xs, 0, 2 * HB + local)

    first = jnp.where(step < half, step * GROUP, local - 2 * HB + step * GROUP)
    weigh_group(idx_ref, rel, first, mass_ref, xs, zt_ref, gram)

    @pl.when(step == pl.num_programs(0) - 1)
    def _():
        i = lax.broadcasted_iota(jnp.int32, (BLK, BLK), 0)
        j = lax.broadcasted_iota(jnp.int32, (BLK, BLK), 1)
        packs = []
        for f in range(FREQ):
            h = gram[f]
            g_real = h[:BLK, :BLK] + h[BLK:, BLK:]
            g_imag = h[:BLK, BLK:] - h[BLK:, :BLK]
            packs.append(jnp.where(i <= j, g_real, g_imag))
        packed_ref[...] = jnp.concatenate(packs, axis=1)


def whiten_packed(packed):
    i = lax.broadcasted_iota(jnp.int32, (BLK, BLK), 0)
    j = lax.broadcasted_iota(jnp.int32, (BLK, BLK), 1)
    turned = packed.T
    g_real = jnp.where(i <= j, packed, turned)
    g_imag = jnp.where(i > j, packed, jnp.where(i < j, -turned, 0.0))
    realified = jnp.concatenate(
        [jnp.concatenate([g_real, -g_imag], 1), jnp.concatenate([g_imag, g_real], 1)], 0
    )
    total = jnp.sum(jnp.sum(realified * realified, axis=1, keepdims=True), axis=0, keepdims=True)
    return realified / jnp.sqrt(total + 1e-06)


def product(a, b):
    return jnp.dot(a, b, precision=lax.Precision.HIGHEST, preferred_element_type=jnp.float32)


def project_kernel(packed_ref, zt_ref, out_ref, zt, out, in_sem, out_sem):
    n = zt.shape[1] // CHUNK

    def fetch(c):
        s = pl.ds(c * CHUNK, CHUNK)
        return pltpu.make_async_copy(zt_ref.at[:, s], zt.at[:, s], in_sem.at[c])

    def send(c):
        s = pl.ds(c * CHUNK, CHUNK)
        return pltpu.make_async_copy(out.at[:, s], out_ref.at[:, s], out_sem.at[c])

    for c in range(n):
        fetch(c).start()
    size = 2 * BLK
    i = lax.broadcasted_iota(jnp.int32, (size, size), 0)
    j = lax.broadcasted_iota(jnp.int32, (size, size), 1)
    eye = jnp.where(i == j, 1.5, 0.0)
    packed = packed_ref[...]
    ys = [whiten_packed(packed[:, f * BLK : (f + 1) * BLK]) for f in range(FREQ)]
    cs = [eye - 0.5 * y for y in ys]
    ys = [product(y, c) for y, c in zip(ys, cs)]
    xs = cs
    for step in range(1, ITERS):
        cs = [eye - 0.5 * product(x, y) for x, y in zip(xs, ys)]
        if step < ITERS - 1:
            ys = [product(y, c) for y, c in zip(ys, cs)]
        xs = [product(c, x) for c, x in zip(cs, xs)]
    projectors = []
    for x in xs:
        top = x.T[:RANK]
        re, im = top[:, :BLK], top[:, BLK:]
        projectors.append(
            jnp.concatenate(
                [jnp.concatenate([re, -im], 1), jnp.concatenate([im, re], 1)], 0
            ).astype(jnp.bfloat16)
        )
    wide = 2 * RANK
    for c in range(n):
        fetch(c).wait()
        s = slice(c * CHUNK, (c + 1) * CHUNK)
        for f in range(FREQ):
            out[f * wide : (f + 1) * wide, s] = jnp.dot(
                projectors[f], zt[f * size : (f + 1) * size, s], preferred_element_type=jnp.float32
            ).astype(jnp.bfloat16)
        send(c).start()
    for c in range(n):
        send(c).wait()


def all_sum(value, axis):
    n = lax.axis_size(axis)
    others = [lax.ppermute(value, axis, [(i, (i + k) % n) for i in range(n)]) for k in range(1, n)]
    for other in others:
        value = value + other
    return value


def local(spectra, mass_blocks, offsets, counts):
    rows, cols = spectra.shape[1:]
    blocks = rows // BS
    slots = mass_blocks.shape[2]
    devices = lax.axis_size(ROW)
    sp = spectra[0].reshape(blocks, BS, cols)
    up = [(i, i + 1) for i in range(devices - 1)]
    down = [(j, i) for i, j in up]
    before = lax.ppermute(sp[blocks - HB :], ROW, up)
    after = lax.ppermute(sp[:HB], ROW, down)

    rel = counts - lax.axis_index(ROW) * rows
    place = jnp.arange(blocks, dtype=jnp.int32)[None, :] + offsets[0].T
    index = jnp.where(place * BS < rel[0], place + HB, blocks + 2 * HB).astype(jnp.int32)
    mass = mass_blocks[0]
    width = GROUP * BS
    inner = blocks - 2 * HB
    xs_shape = pltpu.VMEM((blocks + 2 * HB + 1, BS, cols), jnp.bfloat16)
    mass_block = (GROUP, slots, BS, BS)
    anywhere = pl.BlockSpec(memory_space=pl.ANY)
    gram_shape = (FREQ, 2 * BLK, 2 * BLK)

    zt, part = pl.pallas_call(
        inner_kernel,
        out_shape=(
            jax.ShapeDtypeStruct((cols, rows), jnp.bfloat16),
            jax.ShapeDtypeStruct(gram_shape, jnp.float32),
        ),
        grid_spec=pltpu.PrefetchScalarGridSpec(
            num_scalar_prefetch=2,
            grid=(inner // GROUP,),
            in_specs=[
                pl.BlockSpec(mass_block, lambda s, *_: (s + HB // GROUP, 0, 0, 0)),
                anywhere,
            ],
            out_specs=[
                pl.BlockSpec((cols, width), lambda s, *_: (0, s + HB // GROUP)),
                pl.BlockSpec(gram_shape, lambda s, *_: (0, 0, 0)),
            ],
            scratch_shapes=[xs_shape, pltpu.SemaphoreType.DMA((1,))],
        ),
        name="inner_rows",
    )(index, rel, mass, sp)

    half = HB // GROUP
    edge_block = lambda s: jnp.where(s < half, s, blocks // GROUP - 2 * half + s)
    zt, packed = pl.pallas_call(
        edge_kernel,
        out_shape=(
            jax.ShapeDtypeStruct((cols, rows), jnp.bfloat16),
            jax.ShapeDtypeStruct((BLK, 2 * BLK), jnp.float32),
        ),
        grid_spec=pltpu.PrefetchScalarGridSpec(
            num_scalar_prefetch=2,
            grid=(2 * half,),
            in_specs=[
                pl.BlockSpec(mass_block, lambda s, *_: (edge_block(s), 0, 0, 0)),
                anywhere,
                anywhere,
                anywhere,
                pl.BlockSpec(gram_shape, lambda s, *_: (0, 0, 0)),
                anywhere,
            ],
            out_specs=[
                pl.BlockSpec((cols, width), lambda s, *_: (0, edge_block(s))),
                pl.BlockSpec((BLK, 2 * BLK), lambda s, *_: (0, 0)),
            ],
            scratch_shapes=[
                xs_shape,
                pltpu.VMEM(gram_shape, jnp.float32),
                pltpu.SemaphoreType.DMA((3,)),
            ],
        ),
        input_output_aliases={7: 0},
        name="edge_rows",
    )(index, rel, mass, sp, before, after, part, zt)

    for axis in ("c", "y", "x", "z"):
        packed = all_sum(packed, axis)

    count = rows // CHUNK
    out_rows = FREQ * 2 * RANK
    modes = pl.pallas_call(
        project_kernel,
        out_shape=jax.ShapeDtypeStruct((out_rows, rows), jnp.bfloat16),
        in_specs=[pl.BlockSpec(memory_space=pltpu.VMEM), anywhere],
        out_specs=anywhere,
        scratch_shapes=[
            pltpu.VMEM((cols, rows), jnp.bfloat16),
            pltpu.VMEM((out_rows, rows), jnp.bfloat16),
            pltpu.SemaphoreType.DMA((count,)),
            pltpu.SemaphoreType.DMA((count,)),
        ],
        name="whiten_project",
    )(packed, zt)
    return modes.T[None]


def solution(mesh):
    finer = Mesh(mesh.devices.reshape(4, 2, 4, 4), ("z", "c", "x", "y"))
    return jax.shard_map(
        local,
        mesh=finer,
        in_specs=(
            P(SUB, ROW, None),
            P(SUB, ROW, None, None, None),
            P(SUB, ROW, None),
            P(SUB),
        ),
        out_specs=P(SUB, ROW, None),
        check_vma=False,
    )
```

time: 271 us -> 86.9 us (0.32)
  matrix products: 88.4 us -> 0 us
  local copies, waits for them, and re-layouts: 83.6 us -> 3.64 us
  Pallas kernels: 0 us -> 33.9 us
  other arithmetic: 29.7 us -> 2 us
  blocking collectives: 16.6 us -> 0 us
  waiting for transfers between devices: 36.7 us -> 25.6 us
  starting transfers between devices: 13.1 us -> 20.2 us
    dot_general x25 -> x0, matrix products: 88.4 us -> none  [the longest x9 76.9 us: weigh_columns(): jnp.einsum('bij,bjc->bic', mass_local[:, slot], picked, preferred_element...]
    gather x9 -> x0, local copies, waits for them, and re-layouts: 50.7 us -> none  [weigh_columns(): picked = jnp.take(blocks, block_index[:, slot], axis=0)]
    pallas_call x0 -> x3, Pallas kernels: none -> 33.9 us  [the longest x1 14.3 us: local(): pl.pallas_call(edge_kernel, out_shape=(jax.ShapeDtypeStruct((cols, rows),...]
    all_to_all x1 -> x0, waiting for transfers between devices: 28.6 us -> none  [copy_for_each(): lax.all_to_all(jnp.broadcast_to(value[None], (devices, *value.shape)), ax...]
    concatenate x1 -> x0, other arithmetic: 23.2 us -> none  [with_halo(): value = jnp.concatenate([before, value, after], axis=dim)]
    ppermute x2 -> x12, waiting for transfers between devices: 8.14 us -> 25.6 us  [the longest x10 14.7 us: all_sum(): lax.ppermute(value, axis, [(i, (i + k) % n) for i in range(n)])]
    all_gather x2 -> x0, blocking collectives: 16.6 us -> none  [merged_by_axis(): pieces = lax.all_gather(value, axis)]
    unnamed x23 -> x6, local copies, waits for them, and re-layouts: 17 us -> 0.98 us
  transfers between devices with their start and end apart: 3 -> 12, of which waited for: 3 -> 10; matrix products, arithmetic and copies ran while one was open for 6% -> 1% of each run, Pallas kernels for 0% -> 15%
where the time goes in v1:
time: 86.9 us; the launch traced here: 86 us
  Pallas kernels  33.9 us (39%)
  waiting for transfers between devices  25.6 us (29%)
  starting transfers between devices  20.2 us (23%)
  local copies, waits for them, and re-layouts  3.64 us (4%)
  other arithmetic  2 us (2%)
    ppermute x10, starting transfers between devices, all_sum(): lax.ppermute(value, axis, [(i, (i + k) % n) for i in range(n)])  15.2 us
    ppermute x10, waiting for transfers between devices, all_sum(): lax.ppermute(value, axis, [(i, (i + k) % n) for i in range(n)])  14.7 us
    pallas_call x1, Pallas kernels, local(): pl.pallas_call(edge_kernel, out_shape=(jax.ShapeDtypeStruct((cols, rows),...  14.3 us
    pallas_call x1, Pallas kernels, local(): pl.pallas_call(inner_kernel, out_shape=(jax.ShapeDtypeStruct((cols, rows)...  13 us
    ppermute x1, waiting for transfers between devices, local(): before = lax.ppermute(sp[blocks - HB:], ROW, up)  7.06 us
    pallas_call x1, Pallas kernels, local(): pl.pallas_call(project_kernel, out_shape=jax.ShapeDtypeStruct((out_rows,...  6.6 us
    ppermute x1, waiting for transfers between devices, local(): after = lax.ppermute(sp[:HB], ROW, down)  3.86 us
    ppermute x1, starting transfers between devices, local(): before = lax.ppermute(sp[blocks - HB:], ROW, up)  3.65 us
  transfers between devices with their start and end apart: 12, of which 10 were waited for; matrix products, arithmetic and copies ran while one was open for 1% of the time, Pallas kernels for 15%

profile of v1, /device:TPU:0, one launch (start us, length us, event | category | flops | bytes accessed | tf_op | source)
XLA Modules:
  0.0 86.0 jit_solution(13062642457607881130)
XLA Ops:
  0.0 2.7 %fusion = (bf16[1,2048,256]{2,1,0:T(8,128)(2,1)S(1)}, bf16[1,2048,256]{2,1,0:T(8,128)(2,1)}) fusion(bf16[1,8192,256]{2,1,0:T(8,128)(2,1)} %param.4), kind=kLoop, calls=%fused_computation.6 | loop fusion | bytes 4194304 | tf_op jit(solution)/shard_map/slice | solution.py:189
  2.7 3.6 %collective-permute-start = (bf16[16,128,256]{2,1,0:T(8,128)(2,1)}, bf16[16,128,256]{2,1,0:T(8,128)(2,1)S(1)}, u32[]{:S(2)}, u32[]{:S(2)}) collective-permute-start(bf16[16,128,256]{2,1,0:T(8,128)(2,1)} %bitcast.5), channel_id=1, source_target_pairs={{0,1},{1,2},{2,3},{3,4},{4,5},{5,6},{6,7},{7,8},{8,9},{9,10},{10,1... | collective-permute-start | bytes 3145736 | tf_op jit(solution)/shard_map/ppermute | solution.py:188
  6.3 1.3 %collective-permute-start.1 = (bf16[16,128,256]{2,1,0:T(8,128)(2,1)S(1)}, bf16[16,128,256]{2,1,0:T(8,128)(2,1)S(1)}, u32[]{:S(2)}, u32[]{:S(2)}) collective-permute-start(bf16[16,128,256]{2,1,0:T(8,128)(2,1)S(1)} %bitcast.19), channel_id=1, source_target_pairs={{1,0},{2,1},{3,2},{4,3},{5,4},{6,5},{7,6},{8,7},{9,8},{10,9},{11,1... | collective-permute-start | bytes 3145736 | tf_op jit(solution)/shard_map/ppermute | solution.py:189
  8.3 0.6 add_select_fusion.idx_ref
  8.9 13.0 %inner_rows.1 = (bf16[256,8192]{1,0:T(8,128)(2,1)}, f32[2,128,128]{2,1,0:T(8,128)}) custom-call(s32[9,64]{1,0:T(8,128)} %add_select_fusion.idx_ref, s32[1]{0:T(128)} %sub.7.rel_ref, bf16[64,9,128,128]{3,2,1,0:T(8,128)(2,1)} %bitcast.15, bf16[64,128,256]{2,1,0:T(8,128)(2,1)} %bitcast.17), custom_call_target="tpu_custom_call" | custom-call | tf_op jit(solution)/shard_map/inner_rows/pallas_call | solution.py:202
  21.9 7.1 %collective-permute-done.prev_ref = bf16[16,128,256]{2,1,0:T(8,128)(2,1)S(1)} collective-permute-done((bf16[16,128,256]{2,1,0:T(8,128)(2,1)}, bf16[16,128,256]{2,1,0:T(8,128)(2,1)S(1)}, u32[]{:S(2)}, u32[]{:S(2)}) %collective-permute-start) | collective-permute-done | bytes 1048608 | tf_op jit(solution)/shard_map/ppermute | solution.py:188
  29.0 3.9 %collective-permute-done.1.next_ref = bf16[16,128,256]{2,1,0:T(8,128)(2,1)S(1)} collective-permute-done((bf16[16,128,256]{2,1,0:T(8,128)(2,1)S(1)}, bf16[16,128,256]{2,1,0:T(8,128)(2,1)S(1)}, u32[]{:S(2)}, u32[]{:S(2)}) %collective-permute-start.1) | collective-permute-done | bytes 1048608 | tf_op jit(solution)/shard_map/ppermute | solution.py:189
  32.8 1.0 %copy-done.1 = bf16[16,128,256]{2,1,0:T(8,128)(2,1)} copy-done((bf16[16,128,256]{2,1,0:T(8,128)(2,1)}, bf16[16,128,256]{2,1,0:T(8,128)(2,1)S(1)}, u32[]{:S(2)}) %copy-start.1) | copy-done | bytes 1048600
  33.8 14.3 %edge_rows.1 = (bf16[256,8192]{1,0:T(8,128)(2,1)}, f32[64,128]{1,0:T(8,128)}) custom-call(s32[9,64]{1,0:T(8,128)} %add_select_fusion.idx_ref, s32[1]{0:T(128)} %sub.7.rel_ref, bf16[64,9,128,128]{3,2,1,0:T(8,128)(2,1)} %bitcast.16, bf16[64,128,256]{2,1,0:T(8,128)(2,1)} %bitcast.18, bf16[16,128,256]{2,1,0:T(8,128)(2,1)} %copy-done, ...), custom_call_target="tpu_custom_call", output_to_operand_aliasing={{0}: (7, {})} | custom-call | tf_op jit(solution)/shard_map/edge_rows/pallas_call | solution.py:226
  48.1 0.1 collective-permute-start.2
  48.2 1.4 %collective-permute-done.2 = f32[64,128]{1,0:T(8,128)S(1)} collective-permute-done((f32[64,128]{1,0:T(8,128)}, f32[64,128]{1,0:T(8,128)S(1)}, u32[]{:S(2)}, u32[]{:S(2)}) %collective-permute-start.2) | collective-permute-done | bytes 32800 | tf_op jit(solution)/shard_map/ppermute | solution.py:174
  49.6 0.8 add.52
  50.3 4.6 %collective-permute-start.5 = (f32[64,128]{1,0:T(8,128)S(1)}, f32[64,128]{1,0:T(8,128)S(1)}, u32[]{:S(2)}, u32[]{:S(2)}) collective-permute-start(f32[64,128]{1,0:T(8,128)S(1)} %add.52), channel_id=1, source_target_pairs={{0,3},{1,0},{2,1},{3,2},{4,7},{5,4},{6,5},{7,6},{8,11},{9,8},{10,9... | collective-permute-start | bytes 98312 | tf_op jit(solution)/shard_map/ppermute | solution.py:174
  55.0 0.0 collective-permute-start.4
  55.0 0.9 %collective-permute-start.3 = (f32[64,128]{1,0:T(8,128)S(1)}, f32[64,128]{1,0:T(8,128)S(1)}, u32[]{:S(2)}, u32[]{:S(2)}) collective-permute-start(f32[64,128]{1,0:T(8,128)S(1)} %add.52), channel_id=1, source_target_pairs={{0,1},{1,2},{2,3},{3,0},{4,5},{5,6},{6,7},{7,4},{8,9},{9,10},{10,1... | collective-permute-start | bytes 98312 | tf_op jit(solution)/shard_map/ppermute | solution.py:174
  55.9 0.7 collective-permute-done.5
  56.6 3.8 %collective-permute-done.4 = f32[64,128]{1,0:T(8,128)S(1)} collective-permute-done((f32[64,128]{1,0:T(8,128)S(1)}, f32[64,128]{1,0:T(8,128)S(1)}, u32[]{:S(2)}, u32[]{:S(2)}) %collective-permute-start.4) | collective-permute-done | bytes 32800 | tf_op jit(solution)/shard_map/ppermute | solution.py:174
  60.4 0.1 collective-permute-done.3
  60.5 1.4 %collective-permute-start.8 = (f32[64,128]{1,0:T(8,128)S(1)}, f32[64,128]{1,0:T(8,128)S(1)}, u32[]{:S(2)}, u32[]{:S(2)}) collective-permute-start(f32[64,128]{1,0:T(8,128)S(1)} %add_add_fusion.2), channel_id=1, source_target_pairs={{0,12},{4,0},{8,4},{12,8},{1,13},{5,1},{9,5},{13,9},{2,14},{6,2},{... | collective-permute-start | bytes 98312 | tf_op jit(solution)/shard_map/ppermute | solution.py:174
  61.9 2.2 %collective-permute-start.7 = (f32[64,128]{1,0:T(8,128)S(1)}, f32[64,128]{1,0:T(8,128)S(1)}, u32[]{:S(2)}, u32[]{:S(2)}) collective-permute-start(f32[64,128]{1,0:T(8,128)S(1)} %add_add_fusion.2), channel_id=1, source_target_pairs={{0,8},{4,12},{8,0},{12,4},{1,9},{5,13},{9,1},{13,5},{2,10},{6,14},... | collective-permute-start | bytes 98312 | tf_op jit(solution)/shard_map/ppermute | solution.py:174
  64.1 0.6 collective-permute-start.6
  64.7 0.0 collective-permute-done.8
  64.7 2.6 %collective-permute-done.7 = f32[64,128]{1,0:T(8,128)S(1)} collective-permute-done((f32[64,128]{1,0:T(8,128)S(1)}, f32[64,128]{1,0:T(8,128)S(1)}, u32[]{:S(2)}, u32[]{:S(2)}) %collective-permute-start.7) | collective-permute-done | bytes 32800 | tf_op jit(solution)/shard_map/ppermute | solution.py:174
  67.3 1.9 %collective-permute-done.6 = f32[64,128]{1,0:T(8,128)S(1)} collective-permute-done((f32[64,128]{1,0:T(8,128)S(1)}, f32[64,128]{1,0:T(8,128)S(1)}, u32[]{:S(2)}, u32[]{:S(2)}) %collective-permute-start.6) | collective-permute-done | bytes 32800 | tf_op jit(solution)/shard_map/ppermute | solution.py:174
  69.2 4.1 %collective-permute-start.11 = (f32[64,128]{1,0:T(8,128)S(1)}, f32[64,128]{1,0:T(8,128)S(1)}, u32[]{:S(2)}, u32[]{:S(2)}) collective-permute-start(f32[64,128]{1,0:T(8,128)S(1)} %add_add_fusion.1), channel_id=1, source_target_pairs={{0,96},{32,0},{64,32},{96,64},{1,97},{33,1},{65,33},{97,65},{2,98}... | collective-permute-start | bytes 98312 | tf_op jit(solution)/shard_map/ppermute | solution.py:174
  73.3 0.0 collective-permute-start.10
  73.3 1.3 %collective-permute-start.9 = (f32[64,128]{1,0:T(8,128)S(1)}, f32[64,128]{1,0:T(8,128)S(1)}, u32[]{:S(2)}, u32[]{:S(2)}) collective-permute-start(f32[64,128]{1,0:T(8,128)S(1)} %add_add_fusion.1), channel_id=1, source_target_pairs={{0,32},{32,64},{64,96},{96,0},{1,33},{33,65},{65,97},{97,1},{2,34}... | collective-permute-start | bytes 98312 | tf_op jit(solution)/shard_map/ppermute | solution.py:174
  74.6 0.3 collective-permute-done.11
  74.9 3.9 %collective-permute-done.10 = f32[64,128]{1,0:T(8,128)S(1)} collective-permute-done((f32[64,128]{1,0:T(8,128)S(1)}, f32[64,128]{1,0:T(8,128)S(1)}, u32[]{:S(2)}, u32[]{:S(2)}) %collective-permute-start.10) | collective-permute-done | bytes 32800 | tf_op jit(solution)/shard_map/ppermute | solution.py:174
  78.8 0.0 collective-permute-done.9
  78.8 0.6 add_add_fusion.packed_ref
  79.4 6.6 %whiten_project.1 = bf16[192,8192]{1,0:T(8,128)(2,1)} custom-call(f32[64,128]{1,0:T(8,128)} %add_add_fusion.packed_ref, bf16[256,8192]{1,0:T(8,128)(2,1)} %get-tuple-element.12.zt_ref), custom_call_target="tpu_custom_call" | custom-call | tf_op jit(solution)/shard_map/whiten_project/pallas_call | solution.py:262
  (7 shorter events, 0.0 us)
Async XLA Ops:
  0.0 8.3 %copy-start.2 = (s32[1,64,9]{1,0,2:T(1,128)S(1)}, s32[1,64,9]{1,0,2:T(1,128)}, u32[]{:S(2)}) copy-start(s32[1,64,9]{1,0,2:T(1,128)} %param.6) | copy-start | bytes 6916
  2.7 26.3 %collective-permute-start = (bf16[16,128,256]{2,1,0:T(8,128)(2,1)}, bf16[16,128,256]{2,1,0:T(8,128)(2,1)S(1)}, u32[]{:S(2)}, u32[]{:S(2)}) collective-permute-start(bf16[16,128,256]{2,1,0:T(8,128)(2,1)} %bitcast.5), channel_id=1, source_target_pairs={{0,1},{1,2},{2,3},{3,4},{4,5},{5,6},{6,7},{7,8},{8,9},{9,10},{10,1... | collective-permute-start | bytes 3145736 | tf_op jit(solution)/shard_map/ppermute | solution.py:188
  6.3 26.5 %collective-permute-start.1 = (bf16[16,128,256]{2,1,0:T(8,128)(2,1)S(1)}, bf16[16,128,256]{2,1,0:T(8,128)(2,1)S(1)}, u32[]{:S(2)}, u32[]{:S(2)}) collective-permute-start(bf16[16,128,256]{2,1,0:T(8,128)(2,1)S(1)} %bitcast.19), channel_id=1, source_target_pairs={{1,0},{2,1},{3,2},{4,3},{5,4},{6,5},{7,6},{8,7},{9,8},{10,9},{11,1... | collective-permute-start | bytes 3145736 | tf_op jit(solution)/shard_map/ppermute | solution.py:189
  29.0 3.9 %copy-start = (bf16[16,128,256]{2,1,0:T(8,128)(2,1)}, bf16[16,128,256]{2,1,0:T(8,128)(2,1)S(1)}, u32[]{:S(2)}) copy-start(bf16[16,128,256]{2,1,0:T(8,128)(2,1)S(1)} %collective-permute-done.prev_ref) | copy-start | bytes 3145732
  32.8 1.0 %copy-start.1 = (bf16[16,128,256]{2,1,0:T(8,128)(2,1)}, bf16[16,128,256]{2,1,0:T(8,128)(2,1)S(1)}, u32[]{:S(2)}) copy-start(bf16[16,128,256]{2,1,0:T(8,128)(2,1)S(1)} %collective-permute-done.1.next_ref) | copy-start | bytes 3145732
  48.1 1.5 %collective-permute-start.2 = (f32[64,128]{1,0:T(8,128)}, f32[64,128]{1,0:T(8,128)S(1)}, u32[]{:S(2)}, u32[]{:S(2)}) collective-permute-start(f32[64,128]{1,0:T(8,128)} %get-tuple-element.11), channel_id=1, source_target_pairs={{0,16},{16,0},{1,17},{17,1},{2,18},{18,2},{3,19},{19,3},{4,20},{20... | collective-permute-start | bytes 98312 | tf_op jit(solution)/shard_map/ppermute | solution.py:174
  50.3 6.2 %collective-permute-start.5 = (f32[64,128]{1,0:T(8,128)S(1)}, f32[64,128]{1,0:T(8,128)S(1)}, u32[]{:S(2)}, u32[]{:S(2)}) collective-permute-start(f32[64,128]{1,0:T(8,128)S(1)} %add.52), channel_id=1, source_target_pairs={{0,3},{1,0},{2,1},{3,2},{4,7},{5,4},{6,5},{7,6},{8,11},{9,8},{10,9... | collective-permute-start | bytes 98312 | tf_op jit(solution)/shard_map/ppermute | solution.py:174
  55.0 5.4 %collective-permute-start.4 = (f32[64,128]{1,0:T(8,128)S(1)}, f32[64,128]{1,0:T(8,128)S(1)}, u32[]{:S(2)}, u32[]{:S(2)}) collective-permute-start(f32[64,128]{1,0:T(8,128)S(1)} %add.52), channel_id=1, source_target_pairs={{0,2},{1,3},{2,0},{3,1},{4,6},{5,7},{6,4},{7,5},{8,10},{9,11},{10,... | collective-permute-start | bytes 98312 | tf_op jit(solution)/shard_map/ppermute | solution.py:174
  55.0 5.5 %collective-permute-start.3 = (f32[64,128]{1,0:T(8,128)S(1)}, f32[64,128]{1,0:T(8,128)S(1)}, u32[]{:S(2)}, u32[]{:S(2)}) collective-permute-start(f32[64,128]{1,0:T(8,128)S(1)} %add.52), channel_id=1, source_target_pairs={{0,1},{1,2},{2,3},{3,0},{4,5},{5,6},{6,7},{7,4},{8,9},{9,10},{10,1... | collective-permute-start | bytes 98312 | tf_op jit(solution)/shard_map/ppermute | solution.py:174
  60.5 4.2 %collective-permute-start.8 = (f32[64,128]{1,0:T(8,128)S(1)}, f32[64,128]{1,0:T(8,128)S(1)}, u32[]{:S(2)}, u32[]{:S(2)}) collective-permute-start(f32[64,128]{1,0:T(8,128)S(1)} %add_add_fusion.2), channel_id=1, source_target_pairs={{0,12},{4,0},{8,4},{12,8},{1,13},{5,1},{9,5},{13,9},{2,14},{6,2},{... | collective-permute-start | bytes 98312 | tf_op jit(solution)/shard_map/ppermute | solution.py:174
  61.9 5.4 %collective-permute-start.7 = (f32[64,128]{1,0:T(8,128)S(1)}, f32[64,128]{1,0:T(8,128)S(1)}, u32[]{:S(2)}, u32[]{:S(2)}) collective-permute-start(f32[64,128]{1,0:T(8,128)S(1)} %add_add_fusion.2), channel_id=1, source_target_pairs={{0,8},{4,12},{8,0},{12,4},{1,9},{5,13},{9,1},{13,5},{2,10},{6,14},... | collective-permute-start | bytes 98312 | tf_op jit(solution)/shard_map/ppermute | solution.py:174
  64.1 5.1 %collective-permute-start.6 = (f32[64,128]{1,0:T(8,128)S(1)}, f32[64,128]{1,0:T(8,128)S(1)}, u32[]{:S(2)}, u32[]{:S(2)}) collective-permute-start(f32[64,128]{1,0:T(8,128)S(1)} %add_add_fusion.2), channel_id=1, source_target_pairs={{0,4},{4,8},{8,12},{12,0},{1,5},{5,9},{9,13},{13,1},{2,6},{6,10},{... | collective-permute-start | bytes 98312 | tf_op jit(solution)/shard_map/ppermute | solution.py:174
  69.2 5.7 %collective-permute-start.11 = (f32[64,128]{1,0:T(8,128)S(1)}, f32[64,128]{1,0:T(8,128)S(1)}, u32[]{:S(2)}, u32[]{:S(2)}) collective-permute-start(f32[64,128]{1,0:T(8,128)S(1)} %add_add_fusion.1), channel_id=1, source_target_pairs={{0,96},{32,0},{64,32},{96,64},{1,97},{33,1},{65,33},{97,65},{2,98}... | collective-permute-start | bytes 98312 | tf_op jit(solution)/shard_map/ppermute | solution.py:174
  73.3 5.5 %collective-permute-start.10 = (f32[64,128]{1,0:T(8,128)S(1)}, f32[64,128]{1,0:T(8,128)S(1)}, u32[]{:S(2)}, u32[]{:S(2)}) collective-permute-start(f32[64,128]{1,0:T(8,128)S(1)} %add_add_fusion.1), channel_id=1, source_target_pairs={{0,64},{32,96},{64,0},{96,32},{1,65},{33,97},{65,1},{97,33},{2,66}... | collective-permute-start | bytes 98312 | tf_op jit(solution)/shard_map/ppermute | solution.py:174
  73.3 5.5 %collective-permute-start.9 = (f32[64,128]{1,0:T(8,128)S(1)}, f32[64,128]{1,0:T(8,128)S(1)}, u32[]{:S(2)}, u32[]{:S(2)}) collective-permute-start(f32[64,128]{1,0:T(8,128)S(1)} %add_add_fusion.1), channel_id=1, source_target_pairs={{0,32},{32,64},{64,96},{96,0},{1,33},{33,65},{65,97},{97,1},{2,34}... | collective-permute-start | bytes 98312 | tf_op jit(solution)/shard_map/ppermute | solution.py:174

commit v2 on v1

v2 whole, which is shorter than its diff:
```python
import functools

import jax
import jax.numpy as jnp
from jax import lax
from jax.experimental import pallas as pl
from jax.experimental.pallas import tpu as pltpu
from jax.sharding import Mesh
from jax.sharding import PartitionSpec as P

BLK = 64
RANK = 48
FREQ = 2
ITERS = 5
HB = 16
BS = 128
GROUP = 4
FAR = 4
CHUNK = 1024
SUB = ("z", "c")
ROW = ("x", "y")


def cut_block(rel, xs, spans):
    end = rel + HB * BS
    cut = lax.shift_right_arithmetic(end, 7)
    kept = jnp.bitwise_and(end, BS - 1)
    inside = functools.reduce(jnp.logical_or, [(cut >= lo) & (cut < hi) for lo, hi in spans])

    @pl.when((kept > 0) & inside)
    def _():
        rows = lax.broadcasted_iota(jnp.int32, xs.shape[1:], 0)
        block = xs[cut]
        xs[cut] = jnp.where(rows < kept, block, jnp.zeros_like(block))


def sender(zt, zt_ref, sem, g):
    s = pl.ds(pl.multiple_of(g * GROUP * BS, GROUP * BS), GROUP * BS)
    return pltpu.make_async_copy(zt.at[:, s], zt_ref.at[:, s], sem.at[g])


def weigh_group(idx_ref, rel, first, g, mass, xs, zt_ref, gram):
    slots = mass.shape[1]
    rows = lax.broadcasted_iota(jnp.int32, (BS, xs.shape[2]), 0)
    parts = []
    for r in range(GROUP):
        b = first + r
        left = jnp.concatenate([mass[r, k] for k in range(slots)], axis=1)
        right = jnp.concatenate([xs[idx_ref[k, b]] for k in range(slots)], axis=0)
        acc = jnp.dot(left, right, preferred_element_type=jnp.float32)
        parts.append(jnp.where(rows < rel - b * BS, acc, 0.0).astype(jnp.bfloat16))
    z = jnp.concatenate(parts, axis=0)
    zt = z.T
    zt_ref[:, pl.ds(pl.multiple_of(g * GROUP * BS, GROUP * BS), GROUP * BS)] = zt
    for f in range(FREQ):
        s = slice(f * 2 * BLK, (f + 1) * 2 * BLK)
        gram[f] += jnp.dot(zt[s], z[:, s], preferred_element_type=jnp.float32)


def inner_kernel(idx_ref, rel_ref, mass_ref, sp_ref, zt_ref, gram_ref, xs, edge, mass, zt, x_sem, sem, edge_sem, out_sem):
    rel = rel_ref[0]
    local = sp_ref.shape[0]
    groups = mass.shape[0] // GROUP

    fetch_x = pltpu.make_async_copy(sp_ref, xs.at[pl.ds(HB, local)], x_sem)

    def fetch(g):
        return pltpu.make_async_copy(
            mass_ref.at[pl.ds(HB + g * GROUP, GROUP)], mass.at[pl.ds(g * GROUP, GROUP)], sem.at[g]
        )

    sides = [
        pltpu.make_async_copy(mass_ref.at[pl.ds(0, HB)], edge.at[pl.ds(0, HB)], edge_sem.at[0]),
        pltpu.make_async_copy(
            mass_ref.at[pl.ds(local - HB, HB)], edge.at[pl.ds(HB, HB)], edge_sem.at[1]
        ),
    ]
    fetch_x.start()
    for g in range(groups):
        fetch(g).start()
    for side in sides:
        side.start()
    gram_ref[...] = jnp.zeros_like(gram_ref)
    spare = xs.shape[0] - 1
    xs[spare] = jnp.zeros(xs.shape[1:], xs.dtype)
    fetch_x.wait()
    cut_block(rel, xs, [(HB, HB + local)])

    @pl.loop(0, groups)
    def _(g):
        fetch(g).wait()
        weigh_group(
            idx_ref, rel, HB + g * GROUP, g, mass.at[pl.ds(g * GROUP, GROUP)], xs, zt, gram_ref
        )
        sender(zt, zt_ref, out_sem, g).start()

    for side in sides:
        side.wait()
    for g in range(groups):
        sender(zt, zt_ref, out_sem, g).wait()


def edge_kernel(
    groups, lo, stride, width, idx_ref, rel_ref, edge, prev_ref, next_ref, part_ref, xs_in, xs, zt_ref, gram_ref, gram, zt, sem, out_sem
):
    del xs_in
    rel = rel_ref[0]
    local = xs.shape[0] - 1 - 2 * HB
    low = 0 if width == FAR else FAR
    high = HB + local + (HB - FAR if width == FAR else 0)
    copies = [
        pltpu.make_async_copy(prev_ref, xs.at[pl.ds(low, width)], sem.at[0]),
        pltpu.make_async_copy(next_ref, xs.at[pl.ds(high, width)], sem.at[1]),
    ]
    for copy in copies:
        copy.start()
    gram[...] = part_ref[...]
    for copy in copies:
        copy.wait()
    cut_block(rel, xs, [(low, low + width), (high, high + width)])

    @pl.loop(0, groups)
    def _(g):
        place = lo + g * stride
        first = jnp.where(place < HB // GROUP, place * GROUP, local - 2 * HB + place * GROUP)
        weigh_group(idx_ref, rel, first, g, edge.at[pl.ds(place * GROUP, GROUP)], xs, zt, gram)
        sender(zt, zt_ref, out_sem, g).start()

    if width == FAR:
        gram_ref[...] = pack(gram)
    else:
        gram_ref[...] = gram[...]
    for g in range(groups):
        sender(zt, zt_ref, out_sem, g).wait()


def pack(gram):
    i = lax.broadcasted_iota(jnp.int32, (BLK, BLK), 0)
    j = lax.broadcasted_iota(jnp.int32, (BLK, BLK), 1)
    packs = []
    for f in range(FREQ):
        h = gram[f]
        g_real = h[:BLK, :BLK] + h[BLK:, BLK:]
        g_imag = h[:BLK, BLK:] - h[BLK:, :BLK]
        packs.append(jnp.where(i <= j, g_real, g_imag))
    return jnp.concatenate(packs, axis=1)


def whiten_packed(packed):
    i = lax.broadcasted_iota(jnp.int32, (BLK, BLK), 0)
    j = lax.broadcasted_iota(jnp.int32, (BLK, BLK), 1)
    turned = packed.T
    g_real = jnp.where(i <= j, packed, turned)
    g_imag = jnp.where(i > j, packed, jnp.where(i < j, -turned, 0.0))
    realified = jnp.concatenate(
        [jnp.concatenate([g_real, -g_imag], 1), jnp.concatenate([g_imag, g_real], 1)], 0
    )
    total = jnp.sum(jnp.sum(realified * realified, axis=1, keepdims=True), axis=0, keepdims=True)
    return realified / jnp.sqrt(total + 1e-06)


def product(a, b):
    return jnp.dot(a, b, precision=lax.Precision.HIGHEST, preferred_element_type=jnp.float32)


def project_kernel(packed_ref, inner_ref, near_ref, far_ref, out_ref, zt, out, in_sem, out_sem):
    n = zt.shape[1] // CHUNK
    halves = lambda ref: [ref.at[:, : ref.shape[1] // 2], ref.at[:, ref.shape[1] // 2 :]]
    (near_low, near_high), (far_low, far_high) = halves(near_ref), halves(far_ref)
    fetches, start = [], 0
    for k, piece in enumerate([far_low, near_low, inner_ref, near_high, far_high]):
        stop = start + piece.shape[1]
        fetches.append(pltpu.make_async_copy(piece, zt.at[:, start:stop], in_sem.at[k]))
        start = stop
    for fetch in fetches:
        fetch.start()

    def send(c):
        s = pl.ds(c * CHUNK, CHUNK)
        return pltpu.make_async_copy(out.at[:, s], out_ref.at[:, s], out_sem.at[c])

    size = 2 * BLK
    i = lax.broadcasted_iota(jnp.int32, (size, size), 0)
    j = lax.broadcasted_iota(jnp.int32, (size, size), 1)
    eye = jnp.where(i == j, 1.5, 0.0)
    packed = packed_ref[...]
    ys = [whiten_packed(packed[:, f * BLK : (f + 1) * BLK]) for f in range(FREQ)]
    cs = [eye - 0.5 * y for y in ys]
    ys = [product(y, c) for y, c in zip(ys, cs)]
    xs = cs
    for step in range(1, ITERS):
        cs = [eye - 0.5 * product(x, y) for x, y in zip(xs, ys)]
        if step < ITERS - 1:
            ys = [product(y, c) for y, c in zip(ys, cs)]
        xs = [product(c, x) for c, x in zip(cs, xs)]
    projectors = []
    for x in xs:
        top = x.T[:RANK]
        re, im = top[:, :BLK], top[:, BLK:]
        projectors.append(
            jnp.concatenate(
                [jnp.concatenate([re, -im], 1), jnp.concatenate([im, re], 1)], 0
            ).astype(jnp.bfloat16)
        )
    for fetch in fetches:
        fetch.wait()
    wide = 2 * RANK
    for c in range(n):
        s = slice(c * CHUNK, (c + 1) * CHUNK)
        for f in range(FREQ):
            out[f * wide : (f + 1) * wide, s] = jnp.dot(
                projectors[f], zt[f * size : (f + 1) * size, s], preferred_element_type=jnp.float32
            ).astype(jnp.bfloat16)
        send(c).start()
    for c in range(n):
        send(c).wait()


def all_sum(value, axis):
    n = lax.axis_size(axis)
    others = [lax.ppermute(value, axis, [(i, (i + k) % n) for i in range(n)]) for k in range(1, n)]
    for other in others:
        value = value + other
    return value


def local(spectra, mass_blocks, offsets, counts):
    rows, cols = spectra.shape[1:]
    blocks = rows // BS
    slots = mass_blocks.shape[2]
    devices = lax.axis_size(ROW)
    sp = spectra[0].reshape(blocks, BS, cols)
    up = [(i, i + 1) for i in range(devices - 1)]
    down = [(j, i) for i, j in up]
    far = HB - FAR
    near_before = lax.ppermute(sp[blocks - far :], ROW, up)
    near_after = lax.ppermute(sp[:far], ROW, down)
    far_before = lax.ppermute(sp[blocks - HB : blocks - far], ROW, up)
    far_after = lax.ppermute(sp[far:HB], ROW, down)

    rel = counts - lax.axis_index(ROW) * rows
    place = jnp.arange(blocks, dtype=jnp.int32)[None, :] + offsets[0].T
    index = jnp.where(place * BS < rel[0], place + HB, blocks + 2 * HB).astype(jnp.int32)
    mass = mass_blocks[0]
    inner = blocks - 2 * HB
    anywhere = pl.BlockSpec(memory_space=pl.ANY)
    scalars = pl.BlockSpec(memory_space=pltpu.SMEM)
    near = pl.BlockSpec(memory_space=pltpu.VMEM)
    gram_shape = (FREQ, 2 * BLK, 2 * BLK)
    xs_type = pltpu.VMEM((blocks + 2 * HB + 1, BS, cols), jnp.bfloat16)
    zt_inner = (cols, inner * BS)
    hold = lambda value: pltpu.with_memory_space_constraint(value, pltpu.VMEM)

    zt_in, part, xs, edge = pl.pallas_call(
        inner_kernel,
        out_shape=(
            pltpu.HBM(zt_inner, jnp.bfloat16),
            pltpu.VMEM(gram_shape, jnp.float32),
            xs_type,
            pltpu.VMEM((2 * HB, slots, BS, BS), jnp.bfloat16),
        ),
        in_specs=[scalars, scalars, anywhere, anywhere],
        out_specs=[anywhere] + [near] * 3,
        scratch_shapes=[
            pltpu.VMEM((inner, slots, BS, BS), jnp.bfloat16),
            pltpu.VMEM(zt_inner, jnp.bfloat16),
            pltpu.SemaphoreType.DMA,
            pltpu.SemaphoreType.DMA((inner // GROUP,)),
            pltpu.SemaphoreType.DMA((2,)),
            pltpu.SemaphoreType.DMA((inner // GROUP,)),
        ],
        compiler_params=pltpu.CompilerParams(vmem_limit_bytes=16 << 20),
        name="inner_rows",
    )(index, rel, pltpu.with_memory_space_constraint(mass, pltpu.HBM), pltpu.with_memory_space_constraint(sp, pltpu.HBM))

    def edges(lo, stride, groups, prev, nxt, start, result, held):
        shape = (cols, groups * GROUP * BS)
        return pl.pallas_call(
            functools.partial(edge_kernel, groups, lo, stride, prev.shape[0]),
            out_shape=(xs_type, pltpu.HBM(shape, jnp.bfloat16), result),
            in_specs=[scalars, scalars, near, anywhere, anywhere, near, near],
            out_specs=[near, anywhere, near],
            scratch_shapes=[
                pltpu.VMEM(gram_shape, jnp.float32),
                pltpu.VMEM(shape, jnp.bfloat16),
                pltpu.SemaphoreType.DMA((2,)),
                pltpu.SemaphoreType.DMA((groups,)),
            ],
            input_output_aliases={6: 0},
            compiler_params=pltpu.CompilerParams(vmem_limit_bytes=10 << 20),
            name="edge_rows",
        )(index, rel, hold(edge), prev, nxt, hold(start), hold(held))

    sides = HB // GROUP
    xs, zt_near, part = edges(
        1, 1, 2 * sides - 2, near_before, near_after, part, pltpu.VMEM(gram_shape, jnp.float32), xs
    )
    _, zt_far, packed = edges(
        0, 2 * sides - 1, 2, far_before, far_after, part, jax.ShapeDtypeStruct((BLK, 2 * BLK), jnp.float32), xs
    )

    for axis in ("c", "y", "x", "z"):
        packed = all_sum(packed, axis)

    count = rows // CHUNK
    out_rows = FREQ * 2 * RANK
    modes = pl.pallas_call(
        project_kernel,
        out_shape=jax.ShapeDtypeStruct((out_rows, rows), jnp.bfloat16),
        in_specs=[near, anywhere, anywhere, anywhere],
        out_specs=anywhere,
        scratch_shapes=[
            pltpu.VMEM((cols, rows), jnp.bfloat16),
            pltpu.VMEM((out_rows, rows), jnp.bfloat16),
            pltpu.SemaphoreType.DMA((5,)),
            pltpu.SemaphoreType.DMA((count,)),
        ],
        name="whiten_project",
    )(packed, zt_in, zt_near, zt_far)
    return modes.T[None]


def solution(mesh):
    finer = Mesh(mesh.devices.reshape(4, 2, 4, 4), ("z", "c", "x", "y"))
    return jax.shard_map(
        local,
        mesh=finer,
        in_specs=(
            P(SUB, ROW, None),
            P(SUB, ROW, None, None, None),
            P(SUB, ROW, None),
            P(SUB),
        ),
        out_specs=P(SUB, ROW, None),
        check_vma=False,
    )
```

time: 86.9 us -> 74.8 us (0.86)
  waiting for transfers between devices: 25.6 us -> 12.5 us
  starting transfers between devices: 20.2 us -> 28.9 us
  Pallas kernels: 33.9 us -> 27.8 us
  other arithmetic: 2 us -> 0.64 us
    ppermute x2 -> x4, waiting for transfers between devices: 10.9 us -> 1.31 us  [the longest x1 1.3 us: local(): near_after = lax.ppermute(sp[:far], ROW, down)]
    pallas_call x2 -> x3, Pallas kernels: 27.3 us -> 21 us  [the longest x1 12.1 us: local(): pl.pallas_call(inner_kernel, out_shape=(pltpu.HBM(zt_inner, jnp.bfloat16)...]
    ppermute x2 -> x4, starting transfers between devices: 4.94 us -> 10.8 us  [the longest x1 4.56 us: local(): far_before = lax.ppermute(sp[blocks - HB:blocks - far], ROW, up)]
    ppermute x10, waiting for transfers between devices: 14.7 us -> 11.2 us  [all_sum(): lax.ppermute(value, axis, [(i, (i + k) % n) for i in range(n)])]
    ppermute x10, starting transfers between devices: 15.2 us -> 18.2 us  [all_sum(): lax.ppermute(value, axis, [(i, (i + k) % n) for i in range(n)])]
    unnamed x6 -> x2, local copies, waits for them, and re-layouts: 0.98 us -> 0.01 us
    slice x1 -> x2, local copies, waits for them, and re-layouts: 2.66 us -> 3.43 us  [the longest x1 2.36 us: local(): near_after = lax.ppermute(sp[:far], ROW, down)]
  transfers between devices with their start and end apart: 12 -> 14, of which waited for: 10 -> 9; matrix products, arithmetic and copies ran while one was open for 1% -> 1% of each run, Pallas kernels for 15% -> 24%
where the time goes in v2:
time: 74.8 us; the launch traced here: 74.1 us
  starting transfers between devices  28.9 us (39%)
  Pallas kernels  27.8 us (37%)
  waiting for transfers between devices  12.5 us (17%)
  local copies, waits for them, and re-layouts  3.43 us (5%)
  between operations  0.78 us (1%)
    ppermute x10, starting transfers between devices, all_sum(): lax.ppermute(value, axis, [(i, (i + k) % n) for i in range(n)])  18.2 us
    pallas_call x1, Pallas kernels, local(): pl.pallas_call(inner_kernel, out_shape=(pltpu.HBM(zt_inner, jnp.bfloat16)...  12.1 us
    ppermute x10, waiting for transfers between devices, all_sum(): lax.ppermute(value, axis, [(i, (i + k) % n) for i in range(n)])  11.2 us
    pallas_call x2, Pallas kernels, edges(): pl.pallas_call(functools.partial(edge_kernel, groups, lo, stride, prev.sh...  8.93 us
    pallas_call x1, Pallas kernels, local(): pl.pallas_call(project_kernel, out_shape=jax.ShapeDtypeStruct((out_rows,...  6.77 us
    ppermute x1, starting transfers between devices, local(): far_before = lax.ppermute(sp[blocks - HB:blocks - far], ROW, up)  4.56 us
    ppermute x1, starting transfers between devices, local(): near_before = lax.ppermute(sp[blocks - far:], ROW, up)  3.63 us
    slice x1, local copies, waits for them, and re-layouts, local(): near_after = lax.ppermute(sp[:far], ROW, down)  2.36 us
  transfers between devices with their start and end apart: 14, of which 9 were waited for; matrix products, arithmetic and copies ran while one was open for 1% of the time, Pallas kernels for 24%

profile of v2, /device:TPU:0, one launch (start us, length us, event | category | flops | bytes accessed | tf_op | source)
XLA Modules:
  0.0 74.1 jit_solution(10963269615837458574)
XLA Ops:
  0.0 2.4 %fusion = (bf16[1,1536,256]{2,1,0:T(8,128)(2,1)S(1)}, bf16[1,1536,256]{2,1,0:T(8,128)(2,1)}) fusion(bf16[1,8192,256]{2,1,0:T(8,128)(2,1)} %param.4), kind=kLoop, calls=%fused_computation.6 | loop fusion | bytes 3145728 | tf_op jit(solution)/shard_map/slice | solution.py:237
  2.4 3.6 %collective-permute-start.2 = (bf16[12,128,256]{2,1,0:T(8,128)(2,1)}, bf16[12,128,256]{2,1,0:T(8,128)(2,1)S(1)}, u32[]{:S(2)}, u32[]{:S(2)}) collective-permute-start(bf16[12,128,256]{2,1,0:T(8,128)(2,1)} %bitcast.7), channel_id=1, source_target_pairs={{0,1},{1,2},{2,3},{3,4},{4,5},{5,6},{6,7},{7,8},{8,9},{9,10},{10,1... | collective-permute-start | bytes 2359304 | tf_op jit(solution)/shard_map/ppermute | solution.py:236
  6.0 1.3 %collective-permute-start.3 = (bf16[12,128,256]{2,1,0:T(8,128)(2,1)S(1)}, bf16[12,128,256]{2,1,0:T(8,128)(2,1)S(1)}, u32[]{:S(2)}, u32[]{:S(2)}) collective-permute-start(bf16[12,128,256]{2,1,0:T(8,128)(2,1)S(1)} %bitcast.19), channel_id=1, source_target_pairs={{1,0},{2,1},{3,2},{4,3},{5,4},{6,5},{7,6},{8,7},{9,8},{10,9},{11,1... | collective-permute-start | bytes 2359304 | tf_op jit(solution)/shard_map/ppermute | solution.py:237
  7.3 1.1 %fusion.1 = (bf16[1,512,256]{2,1,0:T(8,128)(2,1)S(1)}, bf16[1,512,256]{2,1,0:T(8,128)(2,1)S(1)}) fusion(bf16[1,8192,256]{2,1,0:T(8,128)(2,1)} %param.4), kind=kLoop, calls=%fused_computation.7 | loop fusion | bytes 1048576 | tf_op jit(solution)/shard_map/slice | solution.py:239
  8.4 4.6 %collective-permute-start = (bf16[4,128,256]{2,1,0:T(8,128)(2,1)S(1)}, bf16[4,128,256]{2,1,0:T(8,128)(2,1)S(1)}, u32[]{:S(2)}, u32[]{:S(2)}) collective-permute-start(bf16[4,128,256]{2,1,0:T(8,128)(2,1)S(1)} %bitcast.21), channel_id=1, source_target_pairs={{0,1},{1,2},{2,3},{3,4},{4,5},{5,6},{6,7},{7,8},{8,9},{9,10},{10,1... | collective-permute-start | bytes 786440 | tf_op jit(solution)/shard_map/ppermute | solution.py:238
  12.9 1.3 %collective-permute-start.1 = (bf16[4,128,256]{2,1,0:T(8,128)(2,1)S(1)}, bf16[4,128,256]{2,1,0:T(8,128)(2,1)S(1)}, u32[]{:S(2)}, u32[]{:S(2)}) collective-permute-start(bf16[4,128,256]{2,1,0:T(8,128)(2,1)S(1)} %bitcast.20), channel_id=1, source_target_pairs={{1,0},{2,1},{3,2},{4,3},{5,4},{6,5},{7,6},{8,7},{9,8},{10,9},{11,1... | collective-permute-start | bytes 786440 | tf_op jit(solution)/shard_map/ppermute | solution.py:239
  14.9 12.1 %inner_rows.1 = (bf16[256,4096]{1,0:T(8,128)(2,1)}, f32[2,128,128]{2,1,0:T(8,128)S(1)}, bf16[97,128,256]{2,1,0:T(8,128)(2,1)S(1)}, bf16[32,9,128,128]{3,2,1,0:T(8,128)(2,1)S(1)}) custom-call(s32[9,64]{1,0:T(8,128)S(1)} %add_select_fusion.idx_ref, s32[1]{0:T(128)} %sub.7.rel_ref, bf16[64,9,128,128]{3,2,1,0:T(8,128)(2,1)} %bitcast.17, ...), custom_call_target="tpu_custom_call" | custom-call | tf_op jit(solution)/shard_map/inner_rows/pallas_call | solution.py:254
  27.0 0.0 collective-permute-done.2.prev_ref
  27.0 1.3 %collective-permute-done.3.next_ref = bf16[12,128,256]{2,1,0:T(8,128)(2,1)S(1)} collective-permute-done((bf16[12,128,256]{2,1,0:T(8,128)(2,1)S(1)}, bf16[12,128,256]{2,1,0:T(8,128)(2,1)S(1)}, u32[]{:S(2)}, u32[]{:S(2)}) %collective-permute-start.3) | collective-permute-done | bytes 786464 | tf_op jit(solution)/shard_map/ppermute | solution.py:237
  28.3 6.1 %edge_rows.2 = (bf16[97,128,256]{2,1,0:T(8,128)(2,1)S(1)}, bf16[256,3072]{1,0:T(8,128)(2,1)}, f32[2,128,128]{2,1,0:T(8,128)S(1)}) custom-call(s32[9,64]{1,0:T(8,128)S(1)} %add_select_fusion.idx_ref, s32[1]{0:T(128)} %sub.7.rel_ref, bf16[32,9,128,128]{3,2,1,0:T(8,128)(2,1)S(1)} %get-tuple-element.14.edge, ...), custom_call_target="tpu_custom_call", output_to_operand_aliasing={{0}: (6, {})} | custom-call | tf_op jit(solution)/shard_map/edge_rows/pallas_call | solution.py:278
  34.4 0.0 collective-permute-done.prev_ref
  34.4 0.0 collective-permute-done.1.next_ref
  34.4 2.9 %edge_rows.3 = (bf16[97,128,256]{2,1,0:T(8,128)(2,1)S(1)}, bf16[256,1024]{1,0:T(8,128)(2,1)}, f32[64,128]{1,0:T(8,128)S(1)}) custom-call(s32[9,64]{1,0:T(8,128)S(1)} %add_select_fusion.idx_ref, s32[1]{0:T(128)} %sub.7.rel_ref, bf16[32,9,128,128]{3,2,1,0:T(8,128)(2,1)S(1)} %get-tuple-element.14.edge, ...), custom_call_target="tpu_custom_call", output_to_operand_aliasing={{0}: (6, {})} | custom-call | tf_op jit(solution)/shard_map/edge_rows/pallas_call | solution.py:278
  37.3 0.1 collective-permute-start.4
  37.4 1.2 %collective-permute-done.4 = f32[64,128]{1,0:T(8,128)S(1)} collective-permute-done((f32[64,128]{1,0:T(8,128)S(1)}, f32[64,128]{1,0:T(8,128)S(1)}, u32[]{:S(2)}, u32[]{:S(2)}) %collective-permute-start.4) | collective-permute-done | bytes 32800 | tf_op jit(solution)/shard_map/ppermute | solution.py:221
  38.6 1.6 %collective-permute-start.5 = (f32[64,128]{1,0:T(8,128)S(1)}, f32[64,128]{1,0:T(8,128)S(1)}, u32[]{:S(2)}, u32[]{:S(2)}) collective-permute-start(f32[64,128]{1,0:T(8,128)S(1)} %add.52), channel_id=1, source_target_pairs={{0,1},{1,2},{2,3},{3,0},{4,5},{5,6},{6,7},{7,4},{8,9},{9,10},{10,1... | collective-permute-start | bytes 98312 | tf_op jit(solution)/shard_map/ppermute | solution.py:221
  40.1 4.6 %collective-permute-start.6 = (f32[64,128]{1,0:T(8,128)S(1)}, f32[64,128]{1,0:T(8,128)S(1)}, u32[]{:S(2)}, u32[]{:S(2)}) collective-permute-start(f32[64,128]{1,0:T(8,128)S(1)} %add.52), channel_id=1, source_target_pairs={{0,2},{1,3},{2,0},{3,1},{4,6},{5,7},{6,4},{7,5},{8,10},{9,11},{10,... | collective-permute-start | bytes 98312 | tf_op jit(solution)/shard_map/ppermute | solution.py:221
  44.7 0.4 collective-permute-done.5
  45.1 1.8 %collective-permute-done.6 = f32[64,128]{1,0:T(8,128)S(1)} collective-permute-done((f32[64,128]{1,0:T(8,128)S(1)}, f32[64,128]{1,0:T(8,128)S(1)}, u32[]{:S(2)}, u32[]{:S(2)}) %collective-permute-start.6) | collective-permute-done | bytes 32800 | tf_op jit(solution)/shard_map/ppermute | solution.py:221
  46.9 1.7 %collective-permute-done.7 = f32[64,128]{1,0:T(8,128)S(1)} collective-permute-done((f32[64,128]{1,0:T(8,128)S(1)}, f32[64,128]{1,0:T(8,128)S(1)}, u32[]{:S(2)}, u32[]{:S(2)}) %collective-permute-start.7) | collective-permute-done | bytes 32800 | tf_op jit(solution)/shard_map/ppermute | solution.py:221
  48.6 3.1 %collective-permute-start.10 = (f32[64,128]{1,0:T(8,128)S(1)}, f32[64,128]{1,0:T(8,128)S(1)}, u32[]{:S(2)}, u32[]{:S(2)}) collective-permute-start(f32[64,128]{1,0:T(8,128)S(1)} %add_add_fusion.2), channel_id=1, source_target_pairs={{0,12},{4,0},{8,4},{12,8},{1,13},{5,1},{9,5},{13,9},{2,14},{6,2},{... | collective-permute-start | bytes 98312 | tf_op jit(solution)/shard_map/ppermute | solution.py:221
  51.7 2.3 %collective-permute-start.9 = (f32[64,128]{1,0:T(8,128)S(1)}, f32[64,128]{1,0:T(8,128)S(1)}, u32[]{:S(2)}, u32[]{:S(2)}) collective-permute-start(f32[64,128]{1,0:T(8,128)S(1)} %add_add_fusion.2), channel_id=1, source_target_pairs={{0,8},{4,12},{8,0},{12,4},{1,9},{5,13},{9,1},{13,5},{2,10},{6,14},... | collective-permute-start | bytes 98312 | tf_op jit(solution)/shard_map/ppermute | solution.py:221
  54.0 2.9 %collective-permute-done.8 = f32[64,128]{1,0:T(8,128)S(1)} collective-permute-done((f32[64,128]{1,0:T(8,128)S(1)}, f32[64,128]{1,0:T(8,128)S(1)}, u32[]{:S(2)}, u32[]{:S(2)}) %collective-permute-start.8) | collective-permute-done | bytes 32800 | tf_op jit(solution)/shard_map/ppermute | solution.py:221
  56.8 0.3 collective-permute-done.9
  57.2 2.0 %collective-permute-start.11 = (f32[64,128]{1,0:T(8,128)S(1)}, f32[64,128]{1,0:T(8,128)S(1)}, u32[]{:S(2)}, u32[]{:S(2)}) collective-permute-start(f32[64,128]{1,0:T(8,128)S(1)} %add_add_fusion.1), channel_id=1, source_target_pairs={{0,32},{32,64},{64,96},{96,0},{1,33},{33,65},{65,97},{97,1},{2,34}... | collective-permute-start | bytes 98312 | tf_op jit(solution)/shard_map/ppermute | solution.py:221
  59.2 3.6 %collective-permute-start.12 = (f32[64,128]{1,0:T(8,128)S(1)}, f32[64,128]{1,0:T(8,128)S(1)}, u32[]{:S(2)}, u32[]{:S(2)}) collective-permute-start(f32[64,128]{1,0:T(8,128)S(1)} %add_add_fusion.1), channel_id=1, source_target_pairs={{0,64},{32,96},{64,0},{96,32},{1,65},{33,97},{65,1},{97,33},{2,66}... | collective-permute-start | bytes 98312 | tf_op jit(solution)/shard_map/ppermute | solution.py:221
  62.8 1.0 %collective-permute-start.13 = (f32[64,128]{1,0:T(8,128)S(1)}, f32[64,128]{1,0:T(8,128)S(1)}, u32[]{:S(2)}, u32[]{:S(2)}) collective-permute-start(f32[64,128]{1,0:T(8,128)S(1)} %add_add_fusion.1), channel_id=1, source_target_pairs={{0,96},{32,0},{64,32},{96,64},{1,97},{33,1},{65,33},{97,65},{2,98}... | collective-permute-start | bytes 98312 | tf_op jit(solution)/shard_map/ppermute | solution.py:221
  63.8 0.0 collective-permute-done.11
  63.8 1.2 %collective-permute-done.12 = f32[64,128]{1,0:T(8,128)S(1)} collective-permute-done((f32[64,128]{1,0:T(8,128)S(1)}, f32[64,128]{1,0:T(8,128)S(1)}, u32[]{:S(2)}, u32[]{:S(2)}) %collective-permute-start.12) | collective-permute-done | bytes 32800 | tf_op jit(solution)/shard_map/ppermute | solution.py:221
  65.0 1.7 %collective-permute-done.13 = f32[64,128]{1,0:T(8,128)S(1)} collective-permute-done((f32[64,128]{1,0:T(8,128)S(1)}, f32[64,128]{1,0:T(8,128)S(1)}, u32[]{:S(2)}, u32[]{:S(2)}) %collective-permute-start.13) | collective-permute-done | bytes 32800 | tf_op jit(solution)/shard_map/ppermute | solution.py:221
  66.7 0.6 add_add_fusion.packed_ref
  67.3 6.8 %whiten_project.1 = bf16[192,8192]{1,0:T(8,128)(2,1)} custom-call(f32[64,128]{1,0:T(8,128)} %add_add_fusion.packed_ref, bf16[256,4096]{1,0:T(8,128)(2,1)} %get-tuple-element.20.inner_ref, bf16[256,3072]{1,0:T(8,128)(2,1)} %get-tuple-element.21.near_ref, bf16[256,1024]{1,0:T(8,128)(2,1)} %get-tuple-element.22.far_ref), custom_call_target="tpu_custom_call" | custom-call | tf_op jit(solution)/shard_map/whiten_project/pallas_call | solution.py:307
  (9 shorter events, 0.0 us)
Async XLA Ops:
  0.0 14.9 %copy-start = (s32[1,64,9]{1,0,2:T(1,128)S(1)}, s32[1,64,9]{1,0,2:T(1,128)}, u32[]{:S(2)}) copy-start(s32[1,64,9]{1,0,2:T(1,128)} %param.6) | copy-start | bytes 6916
  2.4 24.6 %collective-permute-start.2 = (bf16[12,128,256]{2,1,0:T(8,128)(2,1)}, bf16[12,128,256]{2,1,0:T(8,128)(2,1)S(1)}, u32[]{:S(2)}, u32[]{:S(2)}) collective-permute-start(bf16[12,128,256]{2,1,0:T(8,128)(2,1)} %bitcast.7), channel_id=1, source_target_pairs={{0,1},{1,2},{2,3},{3,4},{4,5},{5,6},{6,7},{7,8},{8,9},{9,10},{10,1... | collective-permute-start | bytes 2359304 | tf_op jit(solution)/shard_map/ppermute | solution.py:236
  6.0 22.3 %collective-permute-start.3 = (bf16[12,128,256]{2,1,0:T(8,128)(2,1)S(1)}, bf16[12,128,256]{2,1,0:T(8,128)(2,1)S(1)}, u32[]{:S(2)}, u32[]{:S(2)}) collective-permute-start(bf16[12,128,256]{2,1,0:T(8,128)(2,1)S(1)} %bitcast.19), channel_id=1, source_target_pairs={{1,0},{2,1},{3,2},{4,3},{5,4},{6,5},{7,6},{8,7},{9,8},{10,9},{11,1... | collective-permute-start | bytes 2359304 | tf_op jit(solution)/shard_map/ppermute | solution.py:237
  8.4 26.0 %collective-permute-start = (bf16[4,128,256]{2,1,0:T(8,128)(2,1)S(1)}, bf16[4,128,256]{2,1,0:T(8,128)(2,1)S(1)}, u32[]{:S(2)}, u32[]{:S(2)}) collective-permute-start(bf16[4,128,256]{2,1,0:T(8,128)(2,1)S(1)} %bitcast.21), channel_id=1, source_target_pairs={{0,1},{1,2},{2,3},{3,4},{4,5},{5,6},{6,7},{7,8},{8,9},{9,10},{10,1... | collective-permute-start | bytes 786440 | tf_op jit(solution)/shard_map/ppermute | solution.py:238
  12.9 21.4 %collective-permute-start.1 = (bf16[4,128,256]{2,1,0:T(8,128)(2,1)S(1)}, bf16[4,128,256]{2,1,0:T(8,128)(2,1)S(1)}, u32[]{:S(2)}, u32[]{:S(2)}) collective-permute-start(bf16[4,128,256]{2,1,0:T(8,128)(2,1)S(1)} %bitcast.20), channel_id=1, source_target_pairs={{1,0},{2,1},{3,2},{4,3},{5,4},{6,5},{7,6},{8,7},{9,8},{10,9},{11,1... | collective-permute-start | bytes 786440 | tf_op jit(solution)/shard_map/ppermute | solution.py:239
  37.3 1.3 %collective-permute-start.4 = (f32[64,128]{1,0:T(8,128)S(1)}, f32[64,128]{1,0:T(8,128)S(1)}, u32[]{:S(2)}, u32[]{:S(2)}) collective-permute-start(f32[64,128]{1,0:T(8,128)S(1)} %get-tuple-element.19), channel_id=1, source_target_pairs={{0,16},{16,0},{1,17},{17,1},{2,18},{18,2},{3,19},{19,3},{4,20},{20... | collective-permute-start | bytes 98312 | tf_op jit(solution)/shard_map/ppermute | solution.py:221
  38.6 6.6 %collective-permute-start.5 = (f32[64,128]{1,0:T(8,128)S(1)}, f32[64,128]{1,0:T(8,128)S(1)}, u32[]{:S(2)}, u32[]{:S(2)}) collective-permute-start(f32[64,128]{1,0:T(8,128)S(1)} %add.52), channel_id=1, source_target_pairs={{0,1},{1,2},{2,3},{3,0},{4,5},{5,6},{6,7},{7,4},{8,9},{9,10},{10,1... | collective-permute-start | bytes 98312 | tf_op jit(solution)/shard_map/ppermute | solution.py:221
  40.1 6.8 %collective-permute-start.6 = (f32[64,128]{1,0:T(8,128)S(1)}, f32[64,128]{1,0:T(8,128)S(1)}, u32[]{:S(2)}, u32[]{:S(2)}) collective-permute-start(f32[64,128]{1,0:T(8,128)S(1)} %add.52), channel_id=1, source_target_pairs={{0,2},{1,3},{2,0},{3,1},{4,6},{5,7},{6,4},{7,5},{8,10},{9,11},{10,... | collective-permute-start | bytes 98312 | tf_op jit(solution)/shard_map/ppermute | solution.py:221
  44.7 3.9 %collective-permute-start.7 = (f32[64,128]{1,0:T(8,128)S(1)}, f32[64,128]{1,0:T(8,128)S(1)}, u32[]{:S(2)}, u32[]{:S(2)}) collective-permute-start(f32[64,128]{1,0:T(8,128)S(1)} %add.52), channel_id=1, source_target_pairs={{0,3},{1,0},{2,1},{3,2},{4,7},{5,4},{6,5},{7,6},{8,11},{9,8},{10,9... | collective-permute-start | bytes 98312 | tf_op jit(solution)/shard_map/ppermute | solution.py:221
  48.6 5.3 %collective-permute-start.10 = (f32[64,128]{1,0:T(8,128)S(1)}, f32[64,128]{1,0:T(8,128)S(1)}, u32[]{:S(2)}, u32[]{:S(2)}) collective-permute-start(f32[64,128]{1,0:T(8,128)S(1)} %add_add_fusion.2), channel_id=1, source_target_pairs={{0,12},{4,0},{8,4},{12,8},{1,13},{5,1},{9,5},{13,9},{2,14},{6,2},{... | collective-permute-start | bytes 98312 | tf_op jit(solution)/shard_map/ppermute | solution.py:221
  51.7 5.1 %collective-permute-start.8 = (f32[64,128]{1,0:T(8,128)S(1)}, f32[64,128]{1,0:T(8,128)S(1)}, u32[]{:S(2)}, u32[]{:S(2)}) collective-permute-start(f32[64,128]{1,0:T(8,128)S(1)} %add_add_fusion.2), channel_id=1, source_target_pairs={{0,4},{4,8},{8,12},{12,0},{1,5},{5,9},{9,13},{13,1},{2,6},{6,10},{... | collective-permute-start | bytes 98312 | tf_op jit(solution)/shard_map/ppermute | solution.py:221
  51.7 5.5 %collective-permute-start.9 = (f32[64,128]{1,0:T(8,128)S(1)}, f32[64,128]{1,0:T(8,128)S(1)}, u32[]{:S(2)}, u32[]{:S(2)}) collective-permute-start(f32[64,128]{1,0:T(8,128)S(1)} %add_add_fusion.2), channel_id=1, source_target_pairs={{0,8},{4,12},{8,0},{12,4},{1,9},{5,13},{9,1},{13,5},{2,10},{6,14},... | collective-permute-start | bytes 98312 | tf_op jit(solution)/shard_map/ppermute | solution.py:221
  57.2 6.6 %collective-permute-start.11 = (f32[64,128]{1,0:T(8,128)S(1)}, f32[64,128]{1,0:T(8,128)S(1)}, u32[]{:S(2)}, u32[]{:S(2)}) collective-permute-start(f32[64,128]{1,0:T(8,128)S(1)} %add_add_fusion.1), channel_id=1, source_target_pairs={{0,32},{32,64},{64,96},{96,0},{1,33},{33,65},{65,97},{97,1},{2,34}... | collective-permute-start | bytes 98312 | tf_op jit(solution)/shard_map/ppermute | solution.py:221
  59.2 5.8 %collective-permute-start.12 = (f32[64,128]{1,0:T(8,128)S(1)}, f32[64,128]{1,0:T(8,128)S(1)}, u32[]{:S(2)}, u32[]{:S(2)}) collective-permute-start(f32[64,128]{1,0:T(8,128)S(1)} %add_add_fusion.1), channel_id=1, source_target_pairs={{0,64},{32,96},{64,0},{96,32},{1,65},{33,97},{65,1},{97,33},{2,66}... | collective-permute-start | bytes 98312 | tf_op jit(solution)/shard_map/ppermute | solution.py:221
  62.8 3.9 %collective-permute-start.13 = (f32[64,128]{1,0:T(8,128)S(1)}, f32[64,128]{1,0:T(8,128)S(1)}, u32[]{:S(2)}, u32[]{:S(2)}) collective-permute-start(f32[64,128]{1,0:T(8,128)S(1)} %add_add_fusion.1), channel_id=1, source_target_pairs={{0,96},{32,0},{64,32},{96,64},{1,97},{33,1},{65,33},{97,65},{2,98}... | collective-permute-start | bytes 98312 | tf_op jit(solution)/shard_map/ppermute | solution.py:221

commit v3 on v2

--- a/solution.py
+++ b/solution.py
@@ -35,8 +35,7 @@
 
 
 def sender(zt, zt_ref, sem, g):
-    s = pl.ds(pl.multiple_of(g * GROUP * BS, GROUP * BS), GROUP * BS)
-    return pltpu.make_async_copy(zt.at[:, s], zt_ref.at[:, s], sem.at[g])
+    return pltpu.make_async_copy(zt.at[g], zt_ref.at[g], sem.at[g])
 
 
 def weigh_group(idx_ref, rel, first, g, mass, xs, zt_ref, gram):
@@ -51,7 +50,7 @@
         parts.append(jnp.where(rows < rel - b * BS, acc, 0.0).astype(jnp.bfloat16))
     z = jnp.concatenate(parts, axis=0)
     zt = z.T
-    zt_ref[:, pl.ds(pl.multiple_of(g * GROUP * BS, GROUP * BS), GROUP * BS)] = zt
+    zt_ref[g] = zt
     for f in range(FREQ):
         s = slice(f * 2 * BLK, (f + 1) * 2 * BLK)
         gram[f] += jnp.dot(zt[s], z[:, s], preferred_element_type=jnp.float32)
@@ -163,14 +162,14 @@
     return jnp.dot(a, b, precision=lax.Precision.HIGHEST, preferred_element_type=jnp.float32)
 
 
-def project_kernel(packed_ref, inner_ref, near_ref, far_ref, out_ref, zt, out, in_sem, out_sem):
-    n = zt.shape[1] // CHUNK
-    halves = lambda ref: [ref.at[:, : ref.shape[1] // 2], ref.at[:, ref.shape[1] // 2 :]]
+def project_kernel(sums, inner_ref, near_ref, far_ref, out_ref, zt, out, in_sem, out_sem):
+    n = out.shape[1] // CHUNK
+    halves = lambda ref: [ref.at[: ref.shape[0] // 2], ref.at[ref.shape[0] // 2 :]]
     (near_low, near_high), (far_low, far_high) = halves(near_ref), halves(far_ref)
     fetches, start = [], 0
     for k, piece in enumerate([far_low, near_low, inner_ref, near_high, far_high]):
-        stop = start + piece.shape[1]
-        fetches.append(pltpu.make_async_copy(piece, zt.at[:, start:stop], in_sem.at[k]))
+        stop = start + piece.shape[0]
+        fetches.append(pltpu.make_async_copy(piece, zt.at[start:stop], in_sem.at[k]))
         start = stop
     for fetch in fetches:
         fetch.start()
@@ -183,7 +182,9 @@
     i = lax.broadcasted_iota(jnp.int32, (size, size), 0)
     j = lax.broadcasted_iota(jnp.int32, (size, size), 1)
     eye = jnp.where(i == j, 1.5, 0.0)
-    packed = packed_ref[...]
+    packed = sums[0][...]
+    for other in sums[1:]:
+        packed = packed + other[...]
     ys = [whiten_packed(packed[:, f * BLK : (f + 1) * BLK]) for f in range(FREQ)]
     cs = [eye - 0.5 * y for y in ys]
     ys = [product(y, c) for y, c in zip(ys, cs)]
@@ -205,23 +206,23 @@
     for fetch in fetches:
         fetch.wait()
     wide = 2 * RANK
+    width = zt.shape[2]
     for c in range(n):
-        s = slice(c * CHUNK, (c + 1) * CHUNK)
-        for f in range(FREQ):
-            out[f * wide : (f + 1) * wide, s] = jnp.dot(
-                projectors[f], zt[f * size : (f + 1) * size, s], preferred_element_type=jnp.float32
-            ).astype(jnp.bfloat16)
+        for g in range(c * CHUNK // width, (c + 1) * CHUNK // width):
+            for f in range(FREQ):
+                out[f * wide : (f + 1) * wide, g * width : (g + 1) * width] = jnp.dot(
+                    projectors[f],
+                    zt[g, f * size : (f + 1) * size],
+                    preferred_element_type=jnp.float32,
+                ).astype(jnp.bfloat16)
         send(c).start()
     for c in range(n):
         send(c).wait()
 
 
-def all_sum(value, axis):
+def others(value, axis):
     n = lax.axis_size(axis)
-    others = [lax.ppermute(value, axis, [(i, (i + k) % n) for i in range(n)]) for k in range(1, n)]
-    for other in others:
-        value = value + other
-    return value
+    return [lax.ppermute(value, axis, [(i, (i + k) % n) for i in range(n)]) for k in range(1, n)]
 
 
 def local(spectra, mass_blocks, offsets, counts):
@@ -248,7 +249,7 @@
     near = pl.BlockSpec(memory_space=pltpu.VMEM)
     gram_shape = (FREQ, 2 * BLK, 2 * BLK)
     xs_type = pltpu.VMEM((blocks + 2 * HB + 1, BS, cols), jnp.bfloat16)
-    zt_inner = (cols, inner * BS)
+    zt_inner = (inner // GROUP, cols, GROUP * BS)
     hold = lambda value: pltpu.with_memory_space_constraint(value, pltpu.VMEM)
 
     zt_in, part, xs, edge = pl.pallas_call(
@@ -274,7 +275,7 @@
     )(index, rel, pltpu.with_memory_space_constraint(mass, pltpu.HBM), pltpu.with_memory_space_constraint(sp, pltpu.HBM))
 
     def edges(lo, stride, groups, prev, nxt, start, result, held):
-        shape = (cols, groups * GROUP * BS)
+        shape = (groups, cols, GROUP * BS)
         return pl.pallas_call(
             functools.partial(edge_kernel, groups, lo, stride, prev.shape[0]),
             out_shape=(xs_type, pltpu.HBM(shape, jnp.bfloat16), result),
@@ -299,24 +300,25 @@
         0, 2 * sides - 1, 2, far_before, far_after, part, jax.ShapeDtypeStruct((BLK, 2 * BLK), jnp.float32), xs
     )
 
-    for axis in ("c", "y", "x", "z"):
-        packed = all_sum(packed, axis)
+    for axis in ("c", "y", "x"):
+        packed = sum(others(packed, axis), packed)
+    sums = [packed, *others(packed, "z")]
 
     count = rows // CHUNK
     out_rows = FREQ * 2 * RANK
     modes = pl.pallas_call(
         project_kernel,
         out_shape=jax.ShapeDtypeStruct((out_rows, rows), jnp.bfloat16),
-        in_specs=[near, anywhere, anywhere, anywhere],
+        in_specs=[[near] * len(sums), anywhere, anywhere, anywhere],
         out_specs=anywhere,
         scratch_shapes=[
-            pltpu.VMEM((cols, rows), jnp.bfloat16),
+            pltpu.VMEM((blocks // GROUP, cols, GROUP * BS), jnp.bfloat16),
             pltpu.VMEM((out_rows, rows), jnp.bfloat16),
             pltpu.SemaphoreType.DMA((5,)),
             pltpu.SemaphoreType.DMA((count,)),
         ],
         name="whiten_project",
-    )(packed, zt_in, zt_near, zt_far)
+    )(sums, zt_in, zt_near, zt_far)
     return modes.T[None]
 
 

time: 74.8 us -> 73.6 us (0.984)
  Pallas kernels: 27.8 us -> 26.6 us
    pallas_call x1, Pallas kernels: 6.77 us -> 5.72 us  [local(): pl.pallas_call(project_kernel, out_shape=jax.ShapeDtypeStruct((out_rows,...]
  transfers between devices with their start and end apart: 14 -> 14, of which waited for: 9 -> 9; matrix products, arithmetic and copies ran while one was open for 1% -> 1% of each run, Pallas kernels for 24% -> 25%
where the time goes in v3:
time: 73.6 us; the launch traced here: 72.9 us
  starting transfers between devices  28.9 us (39%)
  Pallas kernels  26.6 us (36%)
  waiting for transfers between devices  12.6 us (17%)
  local copies, waits for them, and re-layouts  4.04 us (5%)
  between operations  0.79 us (1%)
    ppermute x10, starting transfers between devices, others(): lax.ppermute(value, axis, [(i, (i + k) % n) for i in range(n)])  18.1 us
    pallas_call x1, Pallas kernels, local(): pl.pallas_call(inner_kernel, out_shape=(pltpu.HBM(zt_inner, jnp.bfloat16)...  12 us
    ppermute x10, waiting for transfers between devices, others(): lax.ppermute(value, axis, [(i, (i + k) % n) for i in range(n)])  11.2 us
    pallas_call x2, Pallas kernels, edges(): pl.pallas_call(functools.partial(edge_kernel, groups, lo, stride, prev.sh...  8.9 us
    pallas_call x1, Pallas kernels, local(): pl.pallas_call(project_kernel, out_shape=jax.ShapeDtypeStruct((out_rows,...  5.72 us
    ppermute x1, starting transfers between devices, local(): far_before = lax.ppermute(sp[blocks - HB:blocks - far], ROW, up)  4.56 us
    ppermute x1, starting transfers between devices, local(): near_before = lax.ppermute(sp[blocks - far:], ROW, up)  3.63 us
    slice x1, local copies, waits for them, and re-layouts, local(): near_after = lax.ppermute(sp[:far], ROW, down)  2.36 us
  transfers between devices with their start and end apart: 14, of which 9 were waited for; matrix products, arithmetic and copies ran while one was open for 1% of the time, Pallas kernels for 25%

profile of v3, /device:TPU:0, one launch (start us, length us, event | category | flops | bytes accessed | tf_op | source)
XLA Modules:
  0.0 72.9 jit_solution(16905768749265302680)
XLA Ops:
  0.0 2.4 %fusion = (bf16[1,1536,256]{2,1,0:T(8,128)(2,1)S(1)}, bf16[1,1536,256]{2,1,0:T(8,128)(2,1)}) fusion(bf16[1,8192,256]{2,1,0:T(8,128)(2,1)} %param.4), kind=kLoop, calls=%fused_computation.5 | loop fusion | bytes 3145728 | tf_op jit(solution)/shard_map/slice | solution.py:238
  2.4 3.6 %collective-permute-start.2 = (bf16[12,128,256]{2,1,0:T(8,128)(2,1)}, bf16[12,128,256]{2,1,0:T(8,128)(2,1)S(1)}, u32[]{:S(2)}, u32[]{:S(2)}) collective-permute-start(bf16[12,128,256]{2,1,0:T(8,128)(2,1)} %bitcast.7), channel_id=1, source_target_pairs={{0,1},{1,2},{2,3},{3,4},{4,5},{5,6},{6,7},{7,8},{8,9},{9,10},{10,1... | collective-permute-start | bytes 2359304 | tf_op jit(solution)/shard_map/ppermute | solution.py:237
  6.0 1.3 %collective-permute-start.3 = (bf16[12,128,256]{2,1,0:T(8,128)(2,1)S(1)}, bf16[12,128,256]{2,1,0:T(8,128)(2,1)S(1)}, u32[]{:S(2)}, u32[]{:S(2)}) collective-permute-start(bf16[12,128,256]{2,1,0:T(8,128)(2,1)S(1)} %bitcast.19), channel_id=1, source_target_pairs={{1,0},{2,1},{3,2},{4,3},{5,4},{6,5},{7,6},{8,7},{9,8},{10,9},{11,1... | collective-permute-start | bytes 2359304 | tf_op jit(solution)/shard_map/ppermute | solution.py:238
  7.3 1.1 %fusion.1 = (bf16[1,512,256]{2,1,0:T(8,128)(2,1)S(1)}, bf16[1,512,256]{2,1,0:T(8,128)(2,1)S(1)}) fusion(bf16[1,8192,256]{2,1,0:T(8,128)(2,1)} %param.4), kind=kLoop, calls=%fused_computation.6 | loop fusion | bytes 1048576 | tf_op jit(solution)/shard_map/slice | solution.py:240
  8.4 4.6 %collective-permute-start = (bf16[4,128,256]{2,1,0:T(8,128)(2,1)S(1)}, bf16[4,128,256]{2,1,0:T(8,128)(2,1)S(1)}, u32[]{:S(2)}, u32[]{:S(2)}) collective-permute-start(bf16[4,128,256]{2,1,0:T(8,128)(2,1)S(1)} %bitcast.21), channel_id=1, source_target_pairs={{0,1},{1,2},{2,3},{3,4},{4,5},{5,6},{6,7},{7,8},{8,9},{9,10},{10,1... | collective-permute-start | bytes 786440 | tf_op jit(solution)/shard_map/ppermute | solution.py:239
  12.9 1.3 %collective-permute-start.1 = (bf16[4,128,256]{2,1,0:T(8,128)(2,1)S(1)}, bf16[4,128,256]{2,1,0:T(8,128)(2,1)S(1)}, u32[]{:S(2)}, u32[]{:S(2)}) collective-permute-start(bf16[4,128,256]{2,1,0:T(8,128)(2,1)S(1)} %bitcast.20), channel_id=1, source_target_pairs={{1,0},{2,1},{3,2},{4,3},{5,4},{6,5},{7,6},{8,7},{9,8},{10,9},{11,1... | collective-permute-start | bytes 786440 | tf_op jit(solution)/shard_map/ppermute | solution.py:240
  14.9 12.0 %inner_rows.1 = (bf16[8,256,512]{2,1,0:T(8,128)(2,1)}, f32[2,128,128]{2,1,0:T(8,128)S(1)}, bf16[97,128,256]{2,1,0:T(8,128)(2,1)S(1)}, bf16[32,9,128,128]{3,2,1,0:T(8,128)(2,1)S(1)}) custom-call(s32[9,64]{1,0:T(8,128)S(1)} %add_select_fusion.idx_ref, s32[1]{0:T(128)} %sub.7.rel_ref, bf16[64,9,128,128]{3,2,1,0:T(8,128)(2,1)} %bitcast.17, ...), custom_call_target="tpu_custom_call" | custom-call | tf_op jit(solution)/shard_map/inner_rows/pallas_call | solution.py:255
  26.9 0.0 collective-permute-done.2.prev_ref
  27.0 1.3 %collective-permute-done.3.next_ref = bf16[12,128,256]{2,1,0:T(8,128)(2,1)S(1)} collective-permute-done((bf16[12,128,256]{2,1,0:T(8,128)(2,1)S(1)}, bf16[12,128,256]{2,1,0:T(8,128)(2,1)S(1)}, u32[]{:S(2)}, u32[]{:S(2)}) %collective-permute-start.3) | collective-permute-done | bytes 786464 | tf_op jit(solution)/shard_map/ppermute | solution.py:238
  28.3 6.0 %edge_rows.2 = (bf16[97,128,256]{2,1,0:T(8,128)(2,1)S(1)}, bf16[6,256,512]{2,1,0:T(8,128)(2,1)}, f32[2,128,128]{2,1,0:T(8,128)S(1)}) custom-call(s32[9,64]{1,0:T(8,128)S(1)} %add_select_fusion.idx_ref, s32[1]{0:T(128)} %sub.7.rel_ref, bf16[32,9,128,128]{3,2,1,0:T(8,128)(2,1)S(1)} %get-tuple-element.14.edge, ...), custom_call_target="tpu_custom_call", output_to_operand_aliasing={{0}: (6, {})} | custom-call | tf_op jit(solution)/shard_map/edge_rows/pallas_call | solution.py:279
  34.4 0.0 collective-permute-done.1.next_ref
  34.4 2.9 %edge_rows.3 = (bf16[97,128,256]{2,1,0:T(8,128)(2,1)S(1)}, bf16[2,256,512]{2,1,0:T(8,128)(2,1)}, f32[64,128]{1,0:T(8,128)S(1)}) custom-call(s32[9,64]{1,0:T(8,128)S(1)} %add_select_fusion.idx_ref, s32[1]{0:T(128)} %sub.7.rel_ref, bf16[32,9,128,128]{3,2,1,0:T(8,128)(2,1)S(1)} %get-tuple-element.14.edge, ...), custom_call_target="tpu_custom_call", output_to_operand_aliasing={{0}: (6, {})} | custom-call | tf_op jit(solution)/shard_map/edge_rows/pallas_call | solution.py:279
  37.2 0.1 collective-permute-start.4
  37.3 1.2 %collective-permute-done.4 = f32[64,128]{1,0:T(8,128)S(1)} collective-permute-done((f32[64,128]{1,0:T(8,128)S(1)}, f32[64,128]{1,0:T(8,128)S(1)}, u32[]{:S(2)}, u32[]{:S(2)}) %collective-permute-start.4) | collective-permute-done | bytes 32800 | tf_op jit(solution)/shard_map/ppermute | solution.py:225
  38.5 1.6 %collective-permute-start.5 = (f32[64,128]{1,0:T(8,128)S(1)}, f32[64,128]{1,0:T(8,128)S(1)}, u32[]{:S(2)}, u32[]{:S(2)}) collective-permute-start(f32[64,128]{1,0:T(8,128)S(1)} %add.43), channel_id=1, source_target_pairs={{0,1},{1,2},{2,3},{3,0},{4,5},{5,6},{6,7},{7,4},{8,9},{9,10},{10,1... | collective-permute-start | bytes 98312 | tf_op jit(solution)/shard_map/ppermute | solution.py:225
  40.1 4.5 %collective-permute-start.6 = (f32[64,128]{1,0:T(8,128)S(1)}, f32[64,128]{1,0:T(8,128)S(1)}, u32[]{:S(2)}, u32[]{:S(2)}) collective-permute-start(f32[64,128]{1,0:T(8,128)S(1)} %add.43), channel_id=1, source_target_pairs={{0,2},{1,3},{2,0},{3,1},{4,6},{5,7},{6,4},{7,5},{8,10},{9,11},{10,... | collective-permute-start | bytes 98312 | tf_op jit(solution)/shard_map/ppermute | solution.py:225
  44.7 0.0 collective-permute-start.7
  44.7 0.4 collective-permute-done.5
  45.1 1.8 %collective-permute-done.6 = f32[64,128]{1,0:T(8,128)S(1)} collective-permute-done((f32[64,128]{1,0:T(8,128)S(1)}, f32[64,128]{1,0:T(8,128)S(1)}, u32[]{:S(2)}, u32[]{:S(2)}) %collective-permute-start.6) | collective-permute-done | bytes 32800 | tf_op jit(solution)/shard_map/ppermute | solution.py:225
  46.9 1.7 %collective-permute-done.7 = f32[64,128]{1,0:T(8,128)S(1)} collective-permute-done((f32[64,128]{1,0:T(8,128)S(1)}, f32[64,128]{1,0:T(8,128)S(1)}, u32[]{:S(2)}, u32[]{:S(2)}) %collective-permute-start.7) | collective-permute-done | bytes 32800 | tf_op jit(solution)/shard_map/ppermute | solution.py:225
  48.6 3.1 %collective-permute-start.10 = (f32[64,128]{1,0:T(8,128)S(1)}, f32[64,128]{1,0:T(8,128)S(1)}, u32[]{:S(2)}, u32[]{:S(2)}) collective-permute-start(f32[64,128]{1,0:T(8,128)S(1)} %add_add_fusion.1), channel_id=1, source_target_pairs={{0,12},{4,0},{8,4},{12,8},{1,13},{5,1},{9,5},{13,9},{2,14},{6,2},{... | collective-permute-start | bytes 98312 | tf_op jit(solution)/shard_map/ppermute | solution.py:225
  51.7 2.3 %collective-permute-start.9 = (f32[64,128]{1,0:T(8,128)S(1)}, f32[64,128]{1,0:T(8,128)S(1)}, u32[]{:S(2)}, u32[]{:S(2)}) collective-permute-start(f32[64,128]{1,0:T(8,128)S(1)} %add_add_fusion.1), channel_id=1, source_target_pairs={{0,8},{4,12},{8,0},{12,4},{1,9},{5,13},{9,1},{13,5},{2,10},{6,14},... | collective-permute-start | bytes 98312 | tf_op jit(solution)/shard_map/ppermute | solution.py:225
  53.9 0.0 collective-permute-done.10
  54.0 2.9 %collective-permute-done.8 = f32[64,128]{1,0:T(8,128)S(1)} collective-permute-done((f32[64,128]{1,0:T(8,128)S(1)}, f32[64,128]{1,0:T(8,128)S(1)}, u32[]{:S(2)}, u32[]{:S(2)}) %collective-permute-start.8) | collective-permute-done | bytes 32800 | tf_op jit(solution)/shard_map/ppermute | solution.py:225
  56.8 0.3 collective-permute-done.9
  57.2 2.0 %collective-permute-start.11 = (f32[64,128]{1,0:T(8,128)S(1)}, f32[64,128]{1,0:T(8,128)S(1)}, u32[]{:S(2)}, u32[]{:S(2)}) collective-permute-start(f32[64,128]{1,0:T(8,128)S(1)} %add_add_fusion.sums_0_), channel_id=1, source_target_pairs={{0,32},{32,64},{64,96},{96,0},{1,33},{33,65},{65,97},{97,1},{2,34}... | collective-permute-start | bytes 98312 | tf_op jit(solution)/shard_map/ppermute | solution.py:225
  59.1 3.6 %collective-permute-start.12 = (f32[64,128]{1,0:T(8,128)S(1)}, f32[64,128]{1,0:T(8,128)S(1)}, u32[]{:S(2)}, u32[]{:S(2)}) collective-permute-start(f32[64,128]{1,0:T(8,128)S(1)} %add_add_fusion.sums_0_), channel_id=1, source_target_pairs={{0,64},{32,96},{64,0},{96,32},{1,65},{33,97},{65,1},{97,33},{2,66}... | collective-permute-start | bytes 98312 | tf_op jit(solution)/shard_map/ppermute | solution.py:225
  62.7 1.0 %collective-permute-start.13 = (f32[64,128]{1,0:T(8,128)S(1)}, f32[64,128]{1,0:T(8,128)S(1)}, u32[]{:S(2)}, u32[]{:S(2)}) collective-permute-start(f32[64,128]{1,0:T(8,128)S(1)} %add_add_fusion.sums_0_), channel_id=1, source_target_pairs={{0,96},{32,0},{64,32},{96,64},{1,97},{33,1},{65,33},{97,65},{2,98}... | collective-permute-start | bytes 98312 | tf_op jit(solution)/shard_map/ppermute | solution.py:225
  63.7 1.2 %collective-permute-done.12.sums_2_ = f32[64,128]{1,0:T(8,128)S(1)} collective-permute-done((f32[64,128]{1,0:T(8,128)S(1)}, f32[64,128]{1,0:T(8,128)S(1)}, u32[]{:S(2)}, u32[]{:S(2)}) %collective-permute-start.12) | collective-permute-done | bytes 32800 | tf_op jit(solution)/shard_map/ppermute | solution.py:225
  64.9 1.7 %collective-permute-done.13.sums_3_ = f32[64,128]{1,0:T(8,128)S(1)} collective-permute-done((f32[64,128]{1,0:T(8,128)S(1)}, f32[64,128]{1,0:T(8,128)S(1)}, u32[]{:S(2)}, u32[]{:S(2)}) %collective-permute-start.13) | collective-permute-done | bytes 32800 | tf_op jit(solution)/shard_map/ppermute | solution.py:225
  66.6 0.6 copy-done.3
  67.2 5.7 %whiten_project.1 = bf16[192,8192]{1,0:T(8,128)(2,1)} custom-call(f32[64,128]{1,0:T(8,128)} %copy-done, f32[64,128]{1,0:T(8,128)} %copy-done.1, f32[64,128]{1,0:T(8,128)} %copy-done.2, f32[64,128]{1,0:T(8,128)} %copy-done.3, bf16[8,256,512]{2,1,0:T(8,128)(2,1)} %get-tuple-element.20.inner_ref, bf16[6,256,512]{2,1,0:T(8,128)(2,1)} %get-tuple-element.21.near_ref, ...), custom_call_target="tpu_custom_call" | custom-call | tf_op jit(solution)/shard_map/whiten_project/pallas_call | solution.py:309
  (16 shorter events, 0.1 us)
Async XLA Ops:
  0.0 14.9 %copy-start.4 = (s32[1,64,9]{1,0,2:T(1,128)S(1)}, s32[1,64,9]{1,0,2:T(1,128)}, u32[]{:S(2)}) copy-start(s32[1,64,9]{1,0,2:T(1,128)} %param.6) | copy-start | bytes 6916
  2.4 24.6 %collective-permute-start.2 = (bf16[12,128,256]{2,1,0:T(8,128)(2,1)}, bf16[12,128,256]{2,1,0:T(8,128)(2,1)S(1)}, u32[]{:S(2)}, u32[]{:S(2)}) collective-permute-start(bf16[12,128,256]{2,1,0:T(8,128)(2,1)} %bitcast.7), channel_id=1, source_target_pairs={{0,1},{1,2},{2,3},{3,4},{4,5},{5,6},{6,7},{7,8},{8,9},{9,10},{10,1... | collective-permute-start | bytes 2359304 | tf_op jit(solution)/shard_map/ppermute | solution.py:237
  6.0 22.3 %collective-permute-start.3 = (bf16[12,128,256]{2,1,0:T(8,128)(2,1)S(1)}, bf16[12,128,256]{2,1,0:T(8,128)(2,1)S(1)}, u32[]{:S(2)}, u32[]{:S(2)}) collective-permute-start(bf16[12,128,256]{2,1,0:T(8,128)(2,1)S(1)} %bitcast.19), channel_id=1, source_target_pairs={{1,0},{2,1},{3,2},{4,3},{5,4},{6,5},{7,6},{8,7},{9,8},{10,9},{11,1... | collective-permute-start | bytes 2359304 | tf_op jit(solution)/shard_map/ppermute | solution.py:238
  8.4 26.0 %collective-permute-start = (bf16[4,128,256]{2,1,0:T(8,128)(2,1)S(1)}, bf16[4,128,256]{2,1,0:T(8,128)(2,1)S(1)}, u32[]{:S(2)}, u32[]{:S(2)}) collective-permute-start(bf16[4,128,256]{2,1,0:T(8,128)(2,1)S(1)} %bitcast.21), channel_id=1, source_target_pairs={{0,1},{1,2},{2,3},{3,4},{4,5},{5,6},{6,7},{7,8},{8,9},{9,10},{10,1... | collective-permute-start | bytes 786440 | tf_op jit(solution)/shard_map/ppermute | solution.py:239
  12.9 21.4 %collective-permute-start.1 = (bf16[4,128,256]{2,1,0:T(8,128)(2,1)S(1)}, bf16[4,128,256]{2,1,0:T(8,128)(2,1)S(1)}, u32[]{:S(2)}, u32[]{:S(2)}) collective-permute-start(bf16[4,128,256]{2,1,0:T(8,128)(2,1)S(1)} %bitcast.20), channel_id=1, source_target_pairs={{1,0},{2,1},{3,2},{4,3},{5,4},{6,5},{7,6},{8,7},{9,8},{10,9},{11,1... | collective-permute-start | bytes 786440 | tf_op jit(solution)/shard_map/ppermute | solution.py:240
  37.2 1.3 %collective-permute-start.4 = (f32[64,128]{1,0:T(8,128)S(1)}, f32[64,128]{1,0:T(8,128)S(1)}, u32[]{:S(2)}, u32[]{:S(2)}) collective-permute-start(f32[64,128]{1,0:T(8,128)S(1)} %get-tuple-element.19), channel_id=1, source_target_pairs={{0,16},{16,0},{1,17},{17,1},{2,18},{18,2},{3,19},{19,3},{4,20},{20... | collective-permute-start | bytes 98312 | tf_op jit(solution)/shard_map/ppermute | solution.py:225
  38.5 6.6 %collective-permute-start.5 = (f32[64,128]{1,0:T(8,128)S(1)}, f32[64,128]{1,0:T(8,128)S(1)}, u32[]{:S(2)}, u32[]{:S(2)}) collective-permute-start(f32[64,128]{1,0:T(8,128)S(1)} %add.43), channel_id=1, source_target_pairs={{0,1},{1,2},{2,3},{3,0},{4,5},{5,6},{6,7},{7,4},{8,9},{9,10},{10,1... | collective-permute-start | bytes 98312 | tf_op jit(solution)/shard_map/ppermute | solution.py:225
  40.1 6.8 %collective-permute-start.6 = (f32[64,128]{1,0:T(8,128)S(1)}, f32[64,128]{1,0:T(8,128)S(1)}, u32[]{:S(2)}, u32[]{:S(2)}) collective-permute-start(f32[64,128]{1,0:T(8,128)S(1)} %add.43), channel_id=1, source_target_pairs={{0,2},{1,3},{2,0},{3,1},{4,6},{5,7},{6,4},{7,5},{8,10},{9,11},{10,... | collective-permute-start | bytes 98312 | tf_op jit(solution)/shard_map/ppermute | solution.py:225
  44.7 3.9 %collective-permute-start.7 = (f32[64,128]{1,0:T(8,128)S(1)}, f32[64,128]{1,0:T(8,128)S(1)}, u32[]{:S(2)}, u32[]{:S(2)}) collective-permute-start(f32[64,128]{1,0:T(8,128)S(1)} %add.43), channel_id=1, source_target_pairs={{0,3},{1,0},{2,1},{3,2},{4,7},{5,4},{6,5},{7,6},{8,11},{9,8},{10,9... | collective-permute-start | bytes 98312 | tf_op jit(solution)/shard_map/ppermute | solution.py:225
  48.6 5.4 %collective-permute-start.10 = (f32[64,128]{1,0:T(8,128)S(1)}, f32[64,128]{1,0:T(8,128)S(1)}, u32[]{:S(2)}, u32[]{:S(2)}) collective-permute-start(f32[64,128]{1,0:T(8,128)S(1)} %add_add_fusion.1), channel_id=1, source_target_pairs={{0,12},{4,0},{8,4},{12,8},{1,13},{5,1},{9,5},{13,9},{2,14},{6,2},{... | collective-permute-start | bytes 98312 | tf_op jit(solution)/shard_map/ppermute | solution.py:225
  51.7 5.1 %collective-permute-start.8 = (f32[64,128]{1,0:T(8,128)S(1)}, f32[64,128]{1,0:T(8,128)S(1)}, u32[]{:S(2)}, u32[]{:S(2)}) collective-permute-start(f32[64,128]{1,0:T(8,128)S(1)} %add_add_fusion.1), channel_id=1, source_target_pairs={{0,4},{4,8},{8,12},{12,0},{1,5},{5,9},{9,13},{13,1},{2,6},{6,10},{... | collective-permute-start | bytes 98312 | tf_op jit(solution)/shard_map/ppermute | solution.py:225
  51.7 5.5 %collective-permute-start.9 = (f32[64,128]{1,0:T(8,128)S(1)}, f32[64,128]{1,0:T(8,128)S(1)}, u32[]{:S(2)}, u32[]{:S(2)}) collective-permute-start(f32[64,128]{1,0:T(8,128)S(1)} %add_add_fusion.1), channel_id=1, source_target_pairs={{0,8},{4,12},{8,0},{12,4},{1,9},{5,13},{9,1},{13,5},{2,10},{6,14},... | collective-permute-start | bytes 98312 | tf_op jit(solution)/shard_map/ppermute | solution.py:225
  57.2 9.5 %copy-start = (f32[64,128]{1,0:T(8,128)}, f32[64,128]{1,0:T(8,128)S(1)}, u32[]{:S(2)}) copy-start(f32[64,128]{1,0:T(8,128)S(1)} %add_add_fusion.sums_0_) | copy-start | bytes 98308
  57.2 6.5 %collective-permute-start.11 = (f32[64,128]{1,0:T(8,128)S(1)}, f32[64,128]{1,0:T(8,128)S(1)}, u32[]{:S(2)}, u32[]{:S(2)}) collective-permute-start(f32[64,128]{1,0:T(8,128)S(1)} %add_add_fusion.sums_0_), channel_id=1, source_target_pairs={{0,32},{32,64},{64,96},{96,0},{1,33},{33,65},{65,97},{97,1},{2,34}... | collective-permute-start | bytes 98312 | tf_op jit(solution)/shard_map/ppermute | solution.py:225
  59.1 5.8 %collective-permute-start.12 = (f32[64,128]{1,0:T(8,128)S(1)}, f32[64,128]{1,0:T(8,128)S(1)}, u32[]{:S(2)}, u32[]{:S(2)}) collective-permute-start(f32[64,128]{1,0:T(8,128)S(1)} %add_add_fusion.sums_0_), channel_id=1, source_target_pairs={{0,64},{32,96},{64,0},{96,32},{1,65},{33,97},{65,1},{97,33},{2,66}... | collective-permute-start | bytes 98312 | tf_op jit(solution)/shard_map/ppermute | solution.py:225
  62.7 3.9 %collective-permute-start.13 = (f32[64,128]{1,0:T(8,128)S(1)}, f32[64,128]{1,0:T(8,128)S(1)}, u32[]{:S(2)}, u32[]{:S(2)}) collective-permute-start(f32[64,128]{1,0:T(8,128)S(1)} %add_add_fusion.sums_0_), channel_id=1, source_target_pairs={{0,96},{32,0},{64,32},{96,64},{1,97},{33,1},{65,33},{97,65},{2,98}... | collective-permute-start | bytes 98312 | tf_op jit(solution)/shard_map/ppermute | solution.py:225
  63.7 2.9 %copy-start.1 = (f32[64,128]{1,0:T(8,128)}, f32[64,128]{1,0:T(8,128)S(1)}, u32[]{:S(2)}) copy-start(f32[64,128]{1,0:T(8,128)S(1)} %collective-permute-done.11.sums_1_) | copy-start | bytes 98308
  64.9 1.7 %copy-start.2 = (f32[64,128]{1,0:T(8,128)}, f32[64,128]{1,0:T(8,128)S(1)}, u32[]{:S(2)}) copy-start(f32[64,128]{1,0:T(8,128)S(1)} %collective-permute-done.12.sums_2_) | copy-start | bytes 98308
  66.6 0.6 copy-start.3

commit v4 on v3

--- a/solution.py
+++ b/solution.py
@@ -317,8 +317,9 @@
             pltpu.SemaphoreType.DMA((5,)),
             pltpu.SemaphoreType.DMA((count,)),
         ],
+        compiler_params=pltpu.CompilerParams(vmem_limit_bytes=12 << 20),
         name="whiten_project",
-    )(sums, zt_in, zt_near, zt_far)
+    )([hold(v) for v in sums], *(pltpu.with_memory_space_constraint(v, pltpu.HBM) for v in (zt_in, zt_near, zt_far)))
     return modes.T[None]
 
 

time: 73.6 us -> 72.2 us (0.981)
    pallas_call x1, Pallas kernels: 5.72 us -> 4.91 us  [local(): pl.pallas_call(project_kernel, out_shape=jax.ShapeDtypeStruct((out_rows,...]
  transfers between devices with their start and end apart: 14 -> 14, of which waited for: 9 -> 9; matrix products, arithmetic and copies ran while one was open for 1% -> 2% of each run, Pallas kernels for 25% -> 25%
where the time goes in v4:
time: 72.2 us; the launch traced here: 71.5 us
  starting transfers between devices  28.9 us (40%)
  Pallas kernels  25.9 us (36%)
  waiting for transfers between devices  12.5 us (17%)
  local copies, waits for them, and re-layouts  3.43 us (5%)
  between operations  0.78 us (1%)
    ppermute x10, starting transfers between devices, others(): lax.ppermute(value, axis, [(i, (i + k) % n) for i in range(n)])  18.2 us
    pallas_call x1, Pallas kernels, local(): pl.pallas_call(inner_kernel, out_shape=(pltpu.HBM(zt_inner, jnp.bfloat16)...  12 us
    ppermute x10, waiting for transfers between devices, others(): lax.ppermute(value, axis, [(i, (i + k) % n) for i in range(n)])  11.1 us
    pallas_call x2, Pallas kernels, edges(): pl.pallas_call(functools.partial(edge_kernel, groups, lo, stride, prev.sh...  8.91 us
    pallas_call x1, Pallas kernels, local(): pl.pallas_call(project_kernel, out_shape=jax.ShapeDtypeStruct((out_rows,...  4.91 us
    ppermute x1, starting transfers between devices, local(): far_before = lax.ppermute(sp[blocks - HB:blocks - far], ROW, up)  4.56 us
    ppermute x1, starting transfers between devices, local(): near_before = lax.ppermute(sp[blocks - far:], ROW, up)  3.63 us
    slice x1, local copies, waits for them, and re-layouts, local(): near_after = lax.ppermute(sp[:far], ROW, down)  2.36 us
  transfers between devices with their start and end apart: 14, of which 9 were waited for; matrix products, arithmetic and copies ran while one was open for 2% of the time, Pallas kernels for 25%

profile of v4, /device:TPU:0, one launch (start us, length us, event | category | flops | bytes accessed | tf_op | source)
XLA Modules:
  0.0 71.5 jit_solution(833210782632696942)
XLA Ops:
  0.0 2.4 %fusion = (bf16[1,1536,256]{2,1,0:T(8,128)(2,1)S(1)}, bf16[1,1536,256]{2,1,0:T(8,128)(2,1)}) fusion(bf16[1,8192,256]{2,1,0:T(8,128)(2,1)} %param.4), kind=kLoop, calls=%fused_computation.5 | loop fusion | bytes 3145728 | tf_op jit(solution)/shard_map/slice | solution.py:238
  2.4 3.6 %collective-permute-start.2 = (bf16[12,128,256]{2,1,0:T(8,128)(2,1)}, bf16[12,128,256]{2,1,0:T(8,128)(2,1)S(1)}, u32[]{:S(2)}, u32[]{:S(2)}) collective-permute-start(bf16[12,128,256]{2,1,0:T(8,128)(2,1)} %bitcast.7), channel_id=1, source_target_pairs={{0,1},{1,2},{2,3},{3,4},{4,5},{5,6},{6,7},{7,8},{8,9},{9,10},{10,1... | collective-permute-start | bytes 2359304 | tf_op jit(solution)/shard_map/ppermute | solution.py:237
  6.0 1.3 %collective-permute-start.3 = (bf16[12,128,256]{2,1,0:T(8,128)(2,1)S(1)}, bf16[12,128,256]{2,1,0:T(8,128)(2,1)S(1)}, u32[]{:S(2)}, u32[]{:S(2)}) collective-permute-start(bf16[12,128,256]{2,1,0:T(8,128)(2,1)S(1)} %bitcast.19), channel_id=1, source_target_pairs={{1,0},{2,1},{3,2},{4,3},{5,4},{6,5},{7,6},{8,7},{9,8},{10,9},{11,1... | collective-permute-start | bytes 2359304 | tf_op jit(solution)/shard_map/ppermute | solution.py:238
  7.3 1.1 %fusion.1 = (bf16[1,512,256]{2,1,0:T(8,128)(2,1)S(1)}, bf16[1,512,256]{2,1,0:T(8,128)(2,1)S(1)}) fusion(bf16[1,8192,256]{2,1,0:T(8,128)(2,1)} %param.4), kind=kLoop, calls=%fused_computation.6 | loop fusion | bytes 1048576 | tf_op jit(solution)/shard_map/slice | solution.py:240
  8.4 4.6 %collective-permute-start = (bf16[4,128,256]{2,1,0:T(8,128)(2,1)S(1)}, bf16[4,128,256]{2,1,0:T(8,128)(2,1)S(1)}, u32[]{:S(2)}, u32[]{:S(2)}) collective-permute-start(bf16[4,128,256]{2,1,0:T(8,128)(2,1)S(1)} %bitcast.21), channel_id=1, source_target_pairs={{0,1},{1,2},{2,3},{3,4},{4,5},{5,6},{6,7},{7,8},{8,9},{9,10},{10,1... | collective-permute-start | bytes 786440 | tf_op jit(solution)/shard_map/ppermute | solution.py:239
  12.9 1.3 %collective-permute-start.1 = (bf16[4,128,256]{2,1,0:T(8,128)(2,1)S(1)}, bf16[4,128,256]{2,1,0:T(8,128)(2,1)S(1)}, u32[]{:S(2)}, u32[]{:S(2)}) collective-permute-start(bf16[4,128,256]{2,1,0:T(8,128)(2,1)S(1)} %bitcast.20), channel_id=1, source_target_pairs={{1,0},{2,1},{3,2},{4,3},{5,4},{6,5},{7,6},{8,7},{9,8},{10,9},{11,1... | collective-permute-start | bytes 786440 | tf_op jit(solution)/shard_map/ppermute | solution.py:240
  14.9 12.0 %inner_rows.1 = (bf16[8,256,512]{2,1,0:T(8,128)(2,1)}, f32[2,128,128]{2,1,0:T(8,128)S(1)}, bf16[97,128,256]{2,1,0:T(8,128)(2,1)S(1)}, bf16[32,9,128,128]{3,2,1,0:T(8,128)(2,1)S(1)}) custom-call(s32[9,64]{1,0:T(8,128)S(1)} %add_select_fusion.idx_ref, s32[1]{0:T(128)} %sub.7.rel_ref, bf16[64,9,128,128]{3,2,1,0:T(8,128)(2,1)} %bitcast.17, ...), custom_call_target="tpu_custom_call" | custom-call | tf_op jit(solution)/shard_map/inner_rows/pallas_call | solution.py:255
  27.0 0.0 collective-permute-done.2.prev_ref
  27.0 1.3 %collective-permute-done.3.next_ref = bf16[12,128,256]{2,1,0:T(8,128)(2,1)S(1)} collective-permute-done((bf16[12,128,256]{2,1,0:T(8,128)(2,1)S(1)}, bf16[12,128,256]{2,1,0:T(8,128)(2,1)S(1)}, u32[]{:S(2)}, u32[]{:S(2)}) %collective-permute-start.3) | collective-permute-done | bytes 786464 | tf_op jit(solution)/shard_map/ppermute | solution.py:238
  28.3 6.0 %edge_rows.2 = (bf16[97,128,256]{2,1,0:T(8,128)(2,1)S(1)}, bf16[6,256,512]{2,1,0:T(8,128)(2,1)}, f32[2,128,128]{2,1,0:T(8,128)S(1)}) custom-call(s32[9,64]{1,0:T(8,128)S(1)} %add_select_fusion.idx_ref, s32[1]{0:T(128)} %sub.7.rel_ref, bf16[32,9,128,128]{3,2,1,0:T(8,128)(2,1)S(1)} %get-tuple-element.14.edge, ...), custom_call_target="tpu_custom_call", output_to_operand_aliasing={{0}: (6, {})} | custom-call | tf_op jit(solution)/shard_map/edge_rows/pallas_call | solution.py:279
  34.3 0.0 collective-permute-done.prev_ref
  34.4 0.0 collective-permute-done.1.next_ref
  34.4 2.9 %edge_rows.3 = (bf16[97,128,256]{2,1,0:T(8,128)(2,1)S(1)}, bf16[2,256,512]{2,1,0:T(8,128)(2,1)}, f32[64,128]{1,0:T(8,128)S(1)}) custom-call(s32[9,64]{1,0:T(8,128)S(1)} %add_select_fusion.idx_ref, s32[1]{0:T(128)} %sub.7.rel_ref, bf16[32,9,128,128]{3,2,1,0:T(8,128)(2,1)S(1)} %get-tuple-element.14.edge, ...), custom_call_target="tpu_custom_call", output_to_operand_aliasing={{0}: (6, {})} | custom-call | tf_op jit(solution)/shard_map/edge_rows/pallas_call | solution.py:279
  37.3 0.1 collective-permute-start.4
  37.3 1.2 %collective-permute-done.4 = f32[64,128]{1,0:T(8,128)S(1)} collective-permute-done((f32[64,128]{1,0:T(8,128)S(1)}, f32[64,128]{1,0:T(8,128)S(1)}, u32[]{:S(2)}, u32[]{:S(2)}) %collective-permute-start.4) | collective-permute-done | bytes 32800 | tf_op jit(solution)/shard_map/ppermute | solution.py:225
  38.5 1.6 %collective-permute-start.5 = (f32[64,128]{1,0:T(8,128)S(1)}, f32[64,128]{1,0:T(8,128)S(1)}, u32[]{:S(2)}, u32[]{:S(2)}) collective-permute-start(f32[64,128]{1,0:T(8,128)S(1)} %add.43), channel_id=1, source_target_pairs={{0,1},{1,2},{2,3},{3,0},{4,5},{5,6},{6,7},{7,4},{8,9},{9,10},{10,1... | collective-permute-start | bytes 98312 | tf_op jit(solution)/shard_map/ppermute | solution.py:225
  40.1 4.6 %collective-permute-start.6 = (f32[64,128]{1,0:T(8,128)S(1)}, f32[64,128]{1,0:T(8,128)S(1)}, u32[]{:S(2)}, u32[]{:S(2)}) collective-permute-start(f32[64,128]{1,0:T(8,128)S(1)} %add.43), channel_id=1, source_target_pairs={{0,2},{1,3},{2,0},{3,1},{4,6},{5,7},{6,4},{7,5},{8,10},{9,11},{10,... | collective-permute-start | bytes 98312 | tf_op jit(solution)/shard_map/ppermute | solution.py:225
  44.7 0.0 collective-permute-start.7
  44.7 0.4 collective-permute-done.5
  45.1 1.8 %collective-permute-done.6 = f32[64,128]{1,0:T(8,128)S(1)} collective-permute-done((f32[64,128]{1,0:T(8,128)S(1)}, f32[64,128]{1,0:T(8,128)S(1)}, u32[]{:S(2)}, u32[]{:S(2)}) %collective-permute-start.6) | collective-permute-done | bytes 32800 | tf_op jit(solution)/shard_map/ppermute | solution.py:225
  46.9 1.7 %collective-permute-done.7 = f32[64,128]{1,0:T(8,128)S(1)} collective-permute-done((f32[64,128]{1,0:T(8,128)S(1)}, f32[64,128]{1,0:T(8,128)S(1)}, u32[]{:S(2)}, u32[]{:S(2)}) %collective-permute-start.7) | collective-permute-done | bytes 32800 | tf_op jit(solution)/shard_map/ppermute | solution.py:225
  48.6 3.1 %collective-permute-start.10 = (f32[64,128]{1,0:T(8,128)S(1)}, f32[64,128]{1,0:T(8,128)S(1)}, u32[]{:S(2)}, u32[]{:S(2)}) collective-permute-start(f32[64,128]{1,0:T(8,128)S(1)} %add_add_fusion.1), channel_id=1, source_target_pairs={{0,12},{4,0},{8,4},{12,8},{1,13},{5,1},{9,5},{13,9},{2,14},{6,2},{... | collective-permute-start | bytes 98312 | tf_op jit(solution)/shard_map/ppermute | solution.py:225
  51.7 0.0 collective-permute-start.8
  51.7 2.3 %collective-permute-start.9 = (f32[64,128]{1,0:T(8,128)S(1)}, f32[64,128]{1,0:T(8,128)S(1)}, u32[]{:S(2)}, u32[]{:S(2)}) collective-permute-start(f32[64,128]{1,0:T(8,128)S(1)} %add_add_fusion.1), channel_id=1, source_target_pairs={{0,8},{4,12},{8,0},{12,4},{1,9},{5,13},{9,1},{13,5},{2,10},{6,14},... | collective-permute-start | bytes 98312 | tf_op jit(solution)/shard_map/ppermute | solution.py:225
  54.0 2.8 %collective-permute-done.8 = f32[64,128]{1,0:T(8,128)S(1)} collective-permute-done((f32[64,128]{1,0:T(8,128)S(1)}, f32[64,128]{1,0:T(8,128)S(1)}, u32[]{:S(2)}, u32[]{:S(2)}) %collective-permute-start.8) | collective-permute-done | bytes 32800 | tf_op jit(solution)/shard_map/ppermute | solution.py:225
  56.8 0.3 collective-permute-done.9
  57.1 2.0 %collective-permute-start.11 = (f32[64,128]{1,0:T(8,128)S(1)}, f32[64,128]{1,0:T(8,128)S(1)}, u32[]{:S(2)}, u32[]{:S(2)}) collective-permute-start(f32[64,128]{1,0:T(8,128)S(1)} %add_add_fusion.sums_0_), channel_id=1, source_target_pairs={{0,32},{32,64},{64,96},{96,0},{1,33},{33,65},{65,97},{97,1},{2,34}... | collective-permute-start | bytes 98312 | tf_op jit(solution)/shard_map/ppermute | solution.py:225
  59.2 3.5 %collective-permute-start.12 = (f32[64,128]{1,0:T(8,128)S(1)}, f32[64,128]{1,0:T(8,128)S(1)}, u32[]{:S(2)}, u32[]{:S(2)}) collective-permute-start(f32[64,128]{1,0:T(8,128)S(1)} %add_add_fusion.sums_0_), channel_id=1, source_target_pairs={{0,64},{32,96},{64,0},{96,32},{1,65},{33,97},{65,1},{97,33},{2,66}... | collective-permute-start | bytes 98312 | tf_op jit(solution)/shard_map/ppermute | solution.py:225
  62.7 1.0 %collective-permute-start.13 = (f32[64,128]{1,0:T(8,128)S(1)}, f32[64,128]{1,0:T(8,128)S(1)}, u32[]{:S(2)}, u32[]{:S(2)}) collective-permute-start(f32[64,128]{1,0:T(8,128)S(1)} %add_add_fusion.sums_0_), channel_id=1, source_target_pairs={{0,96},{32,0},{64,32},{96,64},{1,97},{33,1},{65,33},{97,65},{2,98}... | collective-permute-start | bytes 98312 | tf_op jit(solution)/shard_map/ppermute | solution.py:225
  63.7 1.2 %collective-permute-done.12.sums_2_ = f32[64,128]{1,0:T(8,128)S(1)} collective-permute-done((f32[64,128]{1,0:T(8,128)S(1)}, f32[64,128]{1,0:T(8,128)S(1)}, u32[]{:S(2)}, u32[]{:S(2)}) %collective-permute-start.12) | collective-permute-done | bytes 32800 | tf_op jit(solution)/shard_map/ppermute | solution.py:225
  64.9 1.7 %collective-permute-done.13.sums_3_ = f32[64,128]{1,0:T(8,128)S(1)} collective-permute-done((f32[64,128]{1,0:T(8,128)S(1)}, f32[64,128]{1,0:T(8,128)S(1)}, u32[]{:S(2)}, u32[]{:S(2)}) %collective-permute-start.13) | collective-permute-done | bytes 32800 | tf_op jit(solution)/shard_map/ppermute | solution.py:225
  66.6 4.9 %whiten_project.1 = bf16[192,8192]{1,0:T(8,128)(2,1)} custom-call(f32[64,128]{1,0:T(8,128)S(1)} %add_add_fusion.sums_0_, f32[64,128]{1,0:T(8,128)S(1)} %collective-permute-done.11.sums_1_, f32[64,128]{1,0:T(8,128)S(1)} %collective-permute-done.12.sums_2_, f32[64,128]{1,0:T(8,128)S(1)} %collective-permute-done.13.sums_3_, ...), custom_call_target="tpu_custom_call" | custom-call | tf_op jit(solution)/shard_map/whiten_project/pallas_call | solution.py:309
  (8 shorter events, 0.0 us)
Async XLA Ops:
  0.0 14.9 %copy-start = (s32[1,64,9]{1,0,2:T(1,128)S(1)}, s32[1,64,9]{1,0,2:T(1,128)}, u32[]{:S(2)}) copy-start(s32[1,64,9]{1,0,2:T(1,128)} %param.6) | copy-start | bytes 6916
  2.4 24.6 %collective-permute-start.2 = (bf16[12,128,256]{2,1,0:T(8,128)(2,1)}, bf16[12,128,256]{2,1,0:T(8,128)(2,1)S(1)}, u32[]{:S(2)}, u32[]{:S(2)}) collective-permute-start(bf16[12,128,256]{2,1,0:T(8,128)(2,1)} %bitcast.7), channel_id=1, source_target_pairs={{0,1},{1,2},{2,3},{3,4},{4,5},{5,6},{6,7},{7,8},{8,9},{9,10},{10,1... | collective-permute-start | bytes 2359304 | tf_op jit(solution)/shard_map/ppermute | solution.py:237
  6.0 22.3 %collective-permute-start.3 = (bf16[12,128,256]{2,1,0:T(8,128)(2,1)S(1)}, bf16[12,128,256]{2,1,0:T(8,128)(2,1)S(1)}, u32[]{:S(2)}, u32[]{:S(2)}) collective-permute-start(bf16[12,128,256]{2,1,0:T(8,128)(2,1)S(1)} %bitcast.19), channel_id=1, source_target_pairs={{1,0},{2,1},{3,2},{4,3},{5,4},{6,5},{7,6},{8,7},{9,8},{10,9},{11,1... | collective-permute-start | bytes 2359304 | tf_op jit(solution)/shard_map/ppermute | solution.py:238
  8.4 26.0 %collective-permute-start = (bf16[4,128,256]{2,1,0:T(8,128)(2,1)S(1)}, bf16[4,128,256]{2,1,0:T(8,128)(2,1)S(1)}, u32[]{:S(2)}, u32[]{:S(2)}) collective-permute-start(bf16[4,128,256]{2,1,0:T(8,128)(2,1)S(1)} %bitcast.21), channel_id=1, source_target_pairs={{0,1},{1,2},{2,3},{3,4},{4,5},{5,6},{6,7},{7,8},{8,9},{9,10},{10,1... | collective-permute-start | bytes 786440 | tf_op jit(solution)/shard_map/ppermute | solution.py:239
  12.9 21.4 %collective-permute-start.1 = (bf16[4,128,256]{2,1,0:T(8,128)(2,1)S(1)}, bf16[4,128,256]{2,1,0:T(8,128)(2,1)S(1)}, u32[]{:S(2)}, u32[]{:S(2)}) collective-permute-start(bf16[4,128,256]{2,1,0:T(8,128)(2,1)S(1)} %bitcast.20), channel_id=1, source_target_pairs={{1,0},{2,1},{3,2},{4,3},{5,4},{6,5},{7,6},{8,7},{9,8},{10,9},{11,1... | collective-permute-start | bytes 786440 | tf_op jit(solution)/shard_map/ppermute | solution.py:240
  37.3 1.3 %collective-permute-start.4 = (f32[64,128]{1,0:T(8,128)S(1)}, f32[64,128]{1,0:T(8,128)S(1)}, u32[]{:S(2)}, u32[]{:S(2)}) collective-permute-start(f32[64,128]{1,0:T(8,128)S(1)} %get-tuple-element.19), channel_id=1, source_target_pairs={{0,16},{16,0},{1,17},{17,1},{2,18},{18,2},{3,19},{19,3},{4,20},{20... | collective-permute-start | bytes 98312 | tf_op jit(solution)/shard_map/ppermute | solution.py:225
  38.5 6.6 %collective-permute-start.5 = (f32[64,128]{1,0:T(8,128)S(1)}, f32[64,128]{1,0:T(8,128)S(1)}, u32[]{:S(2)}, u32[]{:S(2)}) collective-permute-start(f32[64,128]{1,0:T(8,128)S(1)} %add.43), channel_id=1, source_target_pairs={{0,1},{1,2},{2,3},{3,0},{4,5},{5,6},{6,7},{7,4},{8,9},{9,10},{10,1... | collective-permute-start | bytes 98312 | tf_op jit(solution)/shard_map/ppermute | solution.py:225
  40.1 6.8 %collective-permute-start.6 = (f32[64,128]{1,0:T(8,128)S(1)}, f32[64,128]{1,0:T(8,128)S(1)}, u32[]{:S(2)}, u32[]{:S(2)}) collective-permute-start(f32[64,128]{1,0:T(8,128)S(1)} %add.43), channel_id=1, source_target_pairs={{0,2},{1,3},{2,0},{3,1},{4,6},{5,7},{6,4},{7,5},{8,10},{9,11},{10,... | collective-permute-start | bytes 98312 | tf_op jit(solution)/shard_map/ppermute | solution.py:225
  44.7 3.9 %collective-permute-start.7 = (f32[64,128]{1,0:T(8,128)S(1)}, f32[64,128]{1,0:T(8,128)S(1)}, u32[]{:S(2)}, u32[]{:S(2)}) collective-permute-start(f32[64,128]{1,0:T(8,128)S(1)} %add.43), channel_id=1, source_target_pairs={{0,3},{1,0},{2,1},{3,2},{4,7},{5,4},{6,5},{7,6},{8,11},{9,8},{10,9... | collective-permute-start | bytes 98312 | tf_op jit(solution)/shard_map/ppermute | solution.py:225
  48.6 5.4 %collective-permute-start.10 = (f32[64,128]{1,0:T(8,128)S(1)}, f32[64,128]{1,0:T(8,128)S(1)}, u32[]{:S(2)}, u32[]{:S(2)}) collective-permute-start(f32[64,128]{1,0:T(8,128)S(1)} %add_add_fusion.1), channel_id=1, source_target_pairs={{0,12},{4,0},{8,4},{12,8},{1,13},{5,1},{9,5},{13,9},{2,14},{6,2},{... | collective-permute-start | bytes 98312 | tf_op jit(solution)/shard_map/ppermute | solution.py:225
  51.7 5.1 %collective-permute-start.8 = (f32[64,128]{1,0:T(8,128)S(1)}, f32[64,128]{1,0:T(8,128)S(1)}, u32[]{:S(2)}, u32[]{:S(2)}) collective-permute-start(f32[64,128]{1,0:T(8,128)S(1)} %add_add_fusion.1), channel_id=1, source_target_pairs={{0,4},{4,8},{8,12},{12,0},{1,5},{5,9},{9,13},{13,1},{2,6},{6,10},{... | collective-permute-start | bytes 98312 | tf_op jit(solution)/shard_map/ppermute | solution.py:225
  51.7 5.5 %collective-permute-start.9 = (f32[64,128]{1,0:T(8,128)S(1)}, f32[64,128]{1,0:T(8,128)S(1)}, u32[]{:S(2)}, u32[]{:S(2)}) collective-permute-start(f32[64,128]{1,0:T(8,128)S(1)} %add_add_fusion.1), channel_id=1, source_target_pairs={{0,8},{4,12},{8,0},{12,4},{1,9},{5,13},{9,1},{13,5},{2,10},{6,14},... | collective-permute-start | bytes 98312 | tf_op jit(solution)/shard_map/ppermute | solution.py:225
  57.1 6.6 %collective-permute-start.11 = (f32[64,128]{1,0:T(8,128)S(1)}, f32[64,128]{1,0:T(8,128)S(1)}, u32[]{:S(2)}, u32[]{:S(2)}) collective-permute-start(f32[64,128]{1,0:T(8,128)S(1)} %add_add_fusion.sums_0_), channel_id=1, source_target_pairs={{0,32},{32,64},{64,96},{96,0},{1,33},{33,65},{65,97},{97,1},{2,34}... | collective-permute-start | bytes 98312 | tf_op jit(solution)/shard_map/ppermute | solution.py:225
  59.2 5.8 %collective-permute-start.12 = (f32[64,128]{1,0:T(8,128)S(1)}, f32[64,128]{1,0:T(8,128)S(1)}, u32[]{:S(2)}, u32[]{:S(2)}) collective-permute-start(f32[64,128]{1,0:T(8,128)S(1)} %add_add_fusion.sums_0_), channel_id=1, source_target_pairs={{0,64},{32,96},{64,0},{96,32},{1,65},{33,97},{65,1},{97,33},{2,66}... | collective-permute-start | bytes 98312 | tf_op jit(solution)/shard_map/ppermute | solution.py:225
  62.7 3.9 %collective-permute-start.13 = (f32[64,128]{1,0:T(8,128)S(1)}, f32[64,128]{1,0:T(8,128)S(1)}, u32[]{:S(2)}, u32[]{:S(2)}) collective-permute-start(f32[64,128]{1,0:T(8,128)S(1)} %add_add_fusion.sums_0_), channel_id=1, source_target_pairs={{0,96},{32,0},{64,32},{96,64},{1,97},{33,1},{65,33},{97,65},{2,98}... | collective-permute-start | bytes 98312 | tf_op jit(solution)/shard_map/ppermute | solution.py:225
